TPU v7x, 256 devices: a whole 4x4x8 slice. The times are simulated.
256 devices in a mesh: pix: 16 (over x, z_hi, core), frm: 16 (over z_lo, y).
Axes of the slice: x: 4, y: 4, z: 8 (z_hi: 2, z_lo: 4; z = z_hi * 4 + z_lo), core: 2. Of those that a mesh axis runs over, the one named last changes fastest.
Arguments:
- movie: bfloat16 [8192, 4096], P('pix', 'frm'), may hold values from -6 to 6
- taps: float32 [257], replicated, may hold values from -0.25 to 0.25
- scale: float32 [8192], P('pix'), may hold values from 0.3 to 3
- base: float32 [8192], P('pix'), may hold values from 0.2 to 1.5
- spatial: float32 [8192, 256], P('pix'), may hold values from 0.005 to 2
- temporal: float32 [256, 4096], P(None, 'frm'), may hold values from 0.01 to 1.1
Outputs:
- spatial_out: float32 [8192, 256], P('pix')
- temporal_out: float32 [256, 4096], P(None, 'frm')
All inputs are finite; a program needn't handle non-finite values.
Results may differ from a plain program's by a relative error of at most 0.0023.
Values may be sent and summed in bfloat16 or wider, within the bound.
A program may use at most 64 MiB of HBM per device.

v0:
```python
import jax
import jax.numpy as jnp
from jax import lax
from jax.sharding import PartitionSpec as P

ROUNDS = 2


epsilon = 1e-06


def in_blocks(shard, dim, size):
    dims = shard.shape
    parts = shard.reshape(*dims[:dim], size, dims[dim] // size, *dims[dim + 1 :])
    return jnp.moveaxis(parts, dim, 0)


def summed_on_arrival(shard, axis, dim):
    size = lax.axis_size(axis)
    parts = lax.all_to_all(in_blocks(shard, dim, size), axis, 0, 0, tiled=True)
    return jnp.sum(parts, axis=0)


def padded_to(lines, size):
    spare = -lines.shape[0] % size
    if not spare:
        return lines
    return jnp.concatenate([lines, jnp.zeros((spare, *lines.shape[1:]), lines.dtype)])


def in_order(parts, dim):
    dims = list(parts.shape[1:])
    dims[dim] *= parts.shape[0]
    return jnp.moveaxis(parts, 0, dim).reshape(dims)


def sent_to_all(shard, axis):
    copies = jnp.broadcast_to(shard, (lax.axis_size(axis), *shard.shape))
    return lax.all_to_all(copies, axis, split_axis=0, concat_axis=0, tiled=True)


def gather_directly(shard, axis, dim):
    return in_order(sent_to_all(shard, axis), dim)


def nested_sum(shard, axes):
    own = summed_on_arrival(padded_to(shard, lax.axis_size(axes)), axes, 0)
    whole = gather_directly(own, axes, 0)
    return whole[: len(shard)].reshape(shard.shape)


def together(arrays, axis):
    ravelled, at, finished = (jnp.concatenate([a.reshape(-1) for a in arrays]), 0, [])
    so_far = nested_sum(ravelled, axis)
    for a in arrays:
        finished.append(so_far[at : at + a.size].reshape(a.shape))
        at += a.size
    return tuple(finished)


def extended(shard, sides, width):
    for axis, dim in sides:
        size, length = (lax.axis_size(axis), shard.shape[dim])
        up = [(i, (i + 1) % size) for i in range(size - 1)]
        down = [(j, i) for i, j in up]
        last = lax.slice_in_dim(shard, length - width, length, axis=dim)
        leading = lax.slice_in_dim(shard, 0, width, axis=dim)
        before = lax.ppermute(last, axis, up)
        after = lax.ppermute(leading, axis, down)
        shard = jnp.concatenate([before, shard, after], axis=dim)
    return shard


def band_matrix(taps, block_len):
    width = taps.shape[0]
    half_width = (width - 1) // 2
    delta = jnp.where(jnp.arange(width, dtype=jnp.int32) == half_width, 1.0, 0.0).astype(
        jnp.float32
    )
    coefs = delta - taps
    period = width + block_len
    padded_row = jnp.concatenate([coefs, jnp.zeros((block_len,), jnp.float32)])
    tiled = jnp.tile(padded_row, block_len)
    skewed = tiled[: block_len * (period - 1)].reshape(block_len, period - 1)
    return skewed.T.astype(jnp.bfloat16)


def detrend(padded, taps, scale, base, frame_count):
    block_len = min(frame_count, 256)
    band = band_matrix(taps, block_len)
    pixel_count = padded.shape[0]

    def one_block(block_id):
        mixed = jnp.dot(padded, band, preferred_element_type=jnp.float32)
        return jnp.maximum(scale[:, None] * mixed + base[:, None], 0.0).astype(jnp.bfloat16)

    blocks = lax.map(one_block, jnp.arange(frame_count // block_len, dtype=jnp.int32))
    return jnp.transpose(blocks, (1, 0, 2)).reshape(pixel_count, frame_count)


def spatial_whole(normalised, spatial_now, temporal_now):
    temporal_copy = temporal_now.astype(jnp.bfloat16)
    numer_part = jnp.dot(normalised, temporal_copy.T, preferred_element_type=jnp.float32)
    gram_part = jnp.dot(temporal_now, temporal_now.T)
    numer, gram = together((numer_part, gram_part), "frm")
    return spatial_now * numer / (jnp.dot(spatial_now, gram) + epsilon)


def temporal_whole(normalised, spatial_now, temporal_now):
    spatial_copy = spatial_now.astype(jnp.bfloat16)
    numer_part = lax.dot_general(
        spatial_copy, normalised, (((0,), (0,)), ((), ())), preferred_element_type=jnp.float32
    )
    gram_part = lax.dot_general(spatial_now, spatial_now, (((0,), (0,)), ((), ())))
    numer, gram = together((numer_part, gram_part), "pix")
    return temporal_now * numer / (jnp.dot(gram, temporal_now) + epsilon)


def on_device(movie, taps, scale, base, spatial, temporal):
    half_width = (taps.shape[0] - 1) // 2
    frame_count = movie.shape[1]
    padded = extended(movie, (("frm", 1),), half_width)
    normalised = detrend(padded, taps, scale, base, frame_count)
    spatial_now = spatial
    temporal_now = temporal
    for round_id in range(ROUNDS):
        spatial_now = spatial_whole(normalised, spatial_now, temporal_now)
        temporal_now = temporal_whole(normalised, spatial_now, temporal_now)
    return (spatial_now, temporal_now)


def solution(mesh):
    placed = (P("pix", "frm"), P(), P("pix"), P("pix"), P("pix", None), P(None, "frm"))
    return jax.shard_map(
        on_device,
        mesh=mesh,
        in_specs=placed,
        out_specs=(P("pix", None), P(None, "frm")),
        check_vma=False,
    )
```

profile of v0, /device:TPU:33, one launch (start us, length us, event | category | flops | bytes accessed | tf_op | source)
XLA Modules:
  0.0 228.5 jit_solution(7832165528207087962)
XLA Ops:
  0.6 1.0 fusion.22
  1.7 3.2 %collective-permute-start = (bf16[512,128]{1,0:T(8,128)(2,1)S(1)}, bf16[512,128]{1,0:T(8,128)(2,1)S(1)}, u32[]{:S(2)}, u32[]{:S(2)}) collective-permute-start(bf16[512,128]{1,0:T(8,128)(2,1)S(1)} %get-tuple-element.34), channel_id=1, source_target_pairs={{0,1},{1,2},{2,3},{3,4},{4,5},{5,6},{6,7},{7,8},{8,9},{9,10},{10,1... | collective-permute-start | bytes 393224 | tf_op jit(solution)/shard_map/ppermute | solution.py:68
  4.9 4.2 %collective-permute-start.1 = (bf16[512,128]{1,0:T(8,128)(2,1)S(1)}, bf16[512,128]{1,0:T(8,128)(2,1)S(1)}, u32[]{:S(2)}, u32[]{:S(2)}) collective-permute-start(bf16[512,128]{1,0:T(8,128)(2,1)S(1)} %get-tuple-element.35), channel_id=1, source_target_pairs={{1,0},{2,1},{3,2},{4,3},{5,4},{6,5},{7,6},{8,7},{9,8},{10,9},{11,1... | collective-permute-start | bytes 393224 | tf_op jit(solution)/shard_map/ppermute | solution.py:69
  9.5 0.6 tile.11
  10.4 0.6 collective-permute-done.1
  11.1 0.3 fusion.5
  12.1 27.4 %all_to_all.60 = f32[16,1,12288]{2,1,0:T(1,128)S(1)} all-to-all(f32[16,1,12288]{2,1,0:T(1,128)S(1)} %bitcast.37), channel_id=1, replica_groups=mesh['pix'=16,'frm'=16] {'frm'}, dimensions={0} | all-to-all | bytes 1572864 | tf_op jit(solution)/shard_map/all_to_all | solution.py:20
  39.5 0.5 reduce_sum.36
  40.0 1.5 broadcast_in_dim.31
  41.5 5.3 %all-to-all-start.1 = ((f32[16,1,12288]{2,1,0:T(1,128)}), f32[16,1,12288]{2,1,0:T(1,128)S(1)}, u32[]{:S(2)}, u32[]{:S(2)}) async-start(f32[16,1,12288]{2,1,0:T(1,128)} %broadcast_in_dim.31), calls=%async_computation.1 | async-start | bytes 1572864 | tf_op jit(solution)/shard_map/all_to_all | solution.py:39
  47.0 19.0 %all-to-all-done.1 = f32[16,1,12288]{2,1,0:T(1,128)S(1)} async-done(((f32[16,1,12288]{2,1,0:T(1,128)}), f32[16,1,12288]{2,1,0:T(1,128)S(1)}, u32[]{:S(2)}, u32[]{:S(2)}) %all-to-all-start.1) | async-done | bytes 786464 | tf_op jit(solution)/shard_map/all_to_all | solution.py:39
  66.0 1.9 reduce.4
  68.1 1.0 copy.36
  69.1 1.3 fusion.2
  71.1 0.5 all_to_all.43
  71.7 30.3 %all_to_all.61 = f32[16,1,8192]{2,1,0:T(1,128)S(1)} all-to-all(f32[16,1,8192]{2,1,0:T(1,128)S(1)} %all_to_all.43), channel_id=1, replica_groups=mesh['pix'=16,'frm'=16] {'pix'}, dimensions={0} | all-to-all | bytes 1048576 | tf_op jit(solution)/shard_map/all_to_all | solution.py:20
  102.3 0.4 broadcast_in_dim.32
  102.7 21.0 %all_to_all.62 = f32[16,1,8192]{2,1,0:T(1,128)S(1)} all-to-all(f32[16,1,8192]{2,1,0:T(1,128)S(1)} %broadcast_in_dim.32), channel_id=1, replica_groups=mesh['pix'=16,'frm'=16] {'pix'}, dimensions={0} | all-to-all | bytes 1048576 | tf_op jit(solution)/shard_map/all_to_all | solution.py:39
  123.7 1.4 slice_reduce_fusion.3
  126.3 23.6 %all_to_all.63 = f32[16,1,12288]{2,1,0:T(1,128)S(1)} all-to-all(f32[16,1,12288]{2,1,0:T(1,128)S(1)} %bitcast.38), channel_id=1, replica_groups=mesh['pix'=16,'frm'=16] {'frm'}, dimensions={0} | all-to-all | bytes 1572864 | tf_op jit(solution)/shard_map/all_to_all | solution.py:20
  149.9 0.5 reduce_sum.38
  150.4 0.6 broadcast_in_dim.33
  151.0 24.7 %all_to_all.64 = f32[16,1,12288]{2,1,0:T(1,128)S(1)} all-to-all(f32[16,1,12288]{2,1,0:T(1,128)S(1)} %broadcast_in_dim.33), channel_id=1, replica_groups=mesh['pix'=16,'frm'=16] {'frm'}, dimensions={0} | all-to-all | bytes 1572864 | tf_op jit(solution)/shard_map/all_to_all | solution.py:39
  175.7 1.9 reduce.7
  178.9 0.5 all_to_all.49
  179.4 24.1 %all_to_all.65 = f32[16,1,8192]{2,1,0:T(1,128)S(1)} all-to-all(f32[16,1,8192]{2,1,0:T(1,128)S(1)} %all_to_all.49), channel_id=1, replica_groups=mesh['pix'=16,'frm'=16] {'pix'}, dimensions={0} | all-to-all | bytes 1048576 | tf_op jit(solution)/shard_map/all_to_all | solution.py:20
  203.9 1.2 broadcast_in_dim.34
  205.1 4.5 %all-to-all-start.7 = ((f32[16,1,8192]{2,1,0:T(1,128)}), f32[16,1,8192]{2,1,0:T(1,128)S(1)}, u32[]{:S(2)}, u32[]{:S(2)}) async-start(f32[16,1,8192]{2,1,0:T(1,128)} %broadcast_in_dim.34), calls=%async_computation.7 | async-start | bytes 1048576 | tf_op jit(solution)/shard_map/all_to_all | solution.py:39
  209.6 1.0 copy.32
  210.6 15.5 %all-to-all-done.7 = f32[16,1,8192]{2,1,0:T(1,128)S(1)} async-done(((f32[16,1,8192]{2,1,0:T(1,128)}), f32[16,1,8192]{2,1,0:T(1,128)S(1)}, u32[]{:S(2)}, u32[]{:S(2)}) %all-to-all-start.7) | async-done | bytes 524320 | tf_op jit(solution)/shard_map/all_to_all | solution.py:39
  226.1 1.4 slice_reduce_fusion.1
  227.6 0.9 fusion.6
  (54 shorter events, 5.6 us)
Async XLA Ops:
  0.6 8.5 %copy-start = (f32[256,256]{1,0:T(8,128)S(1)}, f32[256,256]{1,0:T(8,128)}, u32[]{:S(2)}) copy-start(f32[256,256]{1,0:T(8,128)} %param.11) | copy-start | bytes 786436
  1.7 7.4 %copy-start.4 = (f32[257]{0:T(512)S(1)}, f32[257]{0:T(512)}, u32[]{:S(2)}) copy-start(f32[257]{0:T(512)} %param.7) | copy-start | bytes 3088
  1.7 8.7 %collective-permute-start = (bf16[512,128]{1,0:T(8,128)(2,1)S(1)}, bf16[512,128]{1,0:T(8,128)(2,1)S(1)}, u32[]{:S(2)}, u32[]{:S(2)}) collective-permute-start(bf16[512,128]{1,0:T(8,128)(2,1)S(1)} %get-tuple-element.34), channel_id=1, source_target_pairs={{0,1},{1,2},{2,3},{3,4},{4,5},{5,6},{6,7},{7,8},{8,9},{9,10},{10,1... | collective-permute-start | bytes 393224 | tf_op jit(solution)/shard_map/ppermute | solution.py:68
  4.9 6.1 %collective-permute-start.1 = (bf16[512,128]{1,0:T(8,128)(2,1)S(1)}, bf16[512,128]{1,0:T(8,128)(2,1)S(1)}, u32[]{:S(2)}, u32[]{:S(2)}) collective-permute-start(bf16[512,128]{1,0:T(8,128)(2,1)S(1)} %get-tuple-element.35), channel_id=1, source_target_pairs={{1,0},{2,1},{3,2},{4,3},{5,4},{6,5},{7,6},{8,7},{9,8},{10,9},{11,1... | collective-permute-start | bytes 393224 | tf_op jit(solution)/shard_map/ppermute | solution.py:69
  10.2 1.0 copy-start.3
  10.2 0.9 copy-start.5
  10.2 0.9 copy-start.6
  41.5 5.3 %copy-start.1 = (f32[512,256]{1,0:T(8,128)S(1)}, f32[512,256]{1,0:T(8,128)}, u32[]{:S(2)}) copy-start(f32[512,256]{1,0:T(8,128)} %param.10) | copy-start | bytes 1572868
  41.5 24.5 %all-to-all-start.1 = ((f32[16,1,12288]{2,1,0:T(1,128)}), f32[16,1,12288]{2,1,0:T(1,128)S(1)}, u32[]{:S(2)}, u32[]{:S(2)}) async-start(f32[16,1,12288]{2,1,0:T(1,128)} %broadcast_in_dim.31), calls=%async_computation.1 | async-start | bytes 1572864 | tf_op jit(solution)/shard_map/all_to_all | solution.py:39
  68.1 1.0 copy-start.2
  205.1 21.0 %all-to-all-start.7 = ((f32[16,1,8192]{2,1,0:T(1,128)}), f32[16,1,8192]{2,1,0:T(1,128)S(1)}, u32[]{:S(2)}, u32[]{:S(2)}) async-start(f32[16,1,8192]{2,1,0:T(1,128)} %broadcast_in_dim.34), calls=%async_computation.7 | async-start | bytes 1048576 | tf_op jit(solution)/shard_map/all_to_all | solution.py:39
where the time goes:
time: 229 us; the launch traced here: 228 us
  blocking collectives  151 us (66%)
  waiting for transfers between devices  35.1 us (15%)
  starting transfers between devices  17.2 us (8%)
  local copies, waits for them, and re-layouts  13.4 us (6%)
  other arithmetic  5.65 us (2%)
  matrix products  4.96 us (2%)
    all_to_all x4, blocking collectives, summed_on_arrival(): parts = lax.all_to_all(in_blocks(shard, dim, size), axis, 0, 0, tiled=True)  105 us
    all_to_all x2, blocking collectives, sent_to_all(): return lax.all_to_all(copies, axis, split_axis=0, concat_axis=0, tiled=True)  45.6 us
    all_to_all x2, waiting for transfers between devices, sent_to_all(): return lax.all_to_all(copies, axis, split_axis=0, concat_axis=0, tiled=True)  34.5 us
    all_to_all x2, starting transfers between devices, sent_to_all(): return lax.all_to_all(copies, axis, split_axis=0, concat_axis=0, tiled=True)  9.8 us
  transfers between devices with their start and end apart: 4, of which 3 were waited for; matrix products, arithmetic and copies ran while one was open for 1% of the time, Pallas kernels for 0%

commit v1 on v0

v1 whole, which is shorter than its diff:
```python
import functools

import jax
import jax.numpy as jnp
from jax import lax
from jax.experimental import pallas as pl
from jax.experimental.pallas import tpu as pltpu
from jax.sharding import PartitionSpec as P

ROUNDS = 2
MESH = pl.DeviceIdType.MESH
F32 = jnp.float32
BF16 = jnp.bfloat16
epsilon = 1e-06

GROUP = 16
CHIPS = 8
PIX = 512
FRM = 256
COMP = 256
ROWS = COMP // GROUP
HALO = 128
TAPS = 257


def frm_steps():
    return sorted(range(1, GROUP), key=lambda k: -(min(k % 4, 4 - k % 4) + k // 4))


def chip_steps():
    return sorted(range(1, CHIPS), key=lambda k: -((k % 2) * 4 + min(k // 2, 4 - k // 2)))


def dot_nn(a, b):
    return lax.dot_general(a, b, (((1,), (0,)), ((), ())), preferred_element_type=F32)


def dot_nt(a, b):
    return lax.dot_general(a, b, (((1,), (1,)), ((), ())), preferred_element_type=F32)


def rows_of(index, count=ROWS):
    return pl.ds(pl.multiple_of(index * count, count), count)


def wait_bytes(ref, sem):
    pltpu.make_async_copy(ref, ref, sem).wait()


def kernel(
    movie_hbm, taps_hbm, scale_hbm, base_hbm, spatial_hbm, temporal_hbm,
    s_out, t_out,
    padded, taps_v, scale_v, base_v, spatial_v, temporal_v,
    coef, norm_t, s_zero_t, s_own, t_own, t_bf,
    gram_part, numer_part, gram_in, numer_in, s_bf,
    mixed_part, core_in, chip_part, chip_in,
    load_sem, halo_send, halo_recv, send_sem, recv_sem,
):
    p = lax.axis_index("pix")
    f = lax.axis_index("frm")
    q, c = lax.div(p, 2), lax.rem(p, 2)

    barrier = pltpu.get_barrier_semaphore()
    for k in range(1, GROUP):
        pl.semaphore_signal(
            barrier, inc=1, device_id=(lax.rem(p + k, GROUP), f), device_id_type=MESH
        )
        pl.semaphore_signal(
            barrier, inc=1, device_id=(p, lax.rem(f + k, GROUP)), device_id_type=MESH
        )

    loads = [
        pltpu.make_async_copy(src, dst, load_sem.at[i])
        for i, (src, dst) in enumerate(
            (
                (movie_hbm, padded.at[:, pl.ds(HALO, FRM)]),
                (temporal_hbm, temporal_v),
                (spatial_hbm, spatial_v),
                (taps_hbm, taps_v),
                (scale_hbm, scale_v),
                (base_hbm, base_v),
            )
        )
    ]
    for copy in loads:
        copy.start()

    def remote(src, dst, phase, target):
        return pltpu.make_async_remote_copy(
            src_ref=src,
            dst_ref=dst,
            send_sem=send_sem.at[phase],
            recv_sem=recv_sem.at[phase],
            device_id=target,
            device_id_type=MESH,
        )

    def frm_scatter(part, inbox, phase):
        for slot, k in enumerate(frm_steps()):
            other = lax.rem(f + k, GROUP)
            remote(part.at[rows_of(other)], inbox.at[slot], phase, (p, other)).start()

    def summed(own, inbox, count):
        total = own
        for slot in range(count):
            total = total + inbox[slot].astype(F32)
        return total

    pl.semaphore_wait(barrier, 2 * (GROUP - 1))
    loads[0].wait()
    to_right = pltpu.make_async_remote_copy(
        src_ref=padded.at[:, pl.ds(FRM, HALO)],
        dst_ref=padded.at[:, pl.ds(0, HALO)],
        send_sem=halo_send.at[0],
        recv_sem=halo_recv.at[0],
        device_id=(p, lax.rem(f + 1, GROUP)),
        device_id_type=MESH,
    )
    to_left = pltpu.make_async_remote_copy(
        src_ref=padded.at[:, pl.ds(HALO, HALO)],
        dst_ref=padded.at[:, pl.ds(HALO + FRM, HALO)],
        send_sem=halo_send.at[1],
        recv_sem=halo_recv.at[1],
        device_id=(p, lax.rem(f + GROUP - 1, GROUP)),
        device_id_type=MESH,
    )

    @pl.when(f < GROUP - 1)
    def _():
        to_right.start()

    @pl.when(f > 0)
    def _():
        to_left.start()

    loads[1].wait()
    t_zero = temporal_v[...].astype(BF16)
    t_bf[0] = t_zero
    gram_part[0] = dot_nt(t_zero, t_zero).astype(BF16)
    frm_scatter(gram_part.at[0], gram_in.at[0], 0)

    @pl.when(f == 0)
    def _():
        padded[:, pl.ds(0, HALO)] = jnp.zeros((PIX, HALO), BF16)

    @pl.when(f == GROUP - 1)
    def _():
        padded[:, pl.ds(HALO + FRM, HALO)] = jnp.zeros((PIX, HALO), BF16)

    for copy in loads[2:]:
        copy.wait()
    coef[...] = jnp.zeros_like(coef)
    centre = lax.broadcasted_iota(jnp.int32, (1, TAPS), 1) == HALO
    coef[:, pl.ds(0, TAPS)] = jnp.where(centre, 1.0, 0.0).astype(F32) - taps_v[...]
    band_t = pltpu.roll(
        jnp.broadcast_to(coef[...], (FRM, 2 * FRM)), 0, 1, stride=1, stride_axis=0
    ).astype(BF16)
    spatial_t = spatial_v[...].T
    s_zero_t[...] = spatial_t
    s_bf[0] = spatial_t.astype(BF16)
    s_own[...] = s_zero_t[rows_of(f), :]
    comp_block = c * CHIPS + q
    t_own[...] = temporal_v[rows_of(comp_block), :]

    @pl.when(f > 0)
    def _():
        to_right.wait_recv()

    @pl.when(f < GROUP - 1)
    def _():
        to_left.wait_recv()

    mixed = dot_nt(band_t, padded[...])
    norm_t[...] = jnp.maximum(scale_v[...] * mixed + base_v[...], 0.0).astype(BF16)

    for r in range(ROUNDS):
        base_phase = 1 + 6 * r
        numer_part[r] = dot_nn(t_bf[r], norm_t[...]).astype(BF16)
        frm_scatter(numer_part.at[r], numer_in.at[r], base_phase)
        if r:
            gram_part[r] = dot_nt(t_bf[r], t_bf[r]).astype(BF16)
            frm_scatter(gram_part.at[r], gram_in.at[r], base_phase + 1)
        gram_phase = base_phase + 1 if r else 0
        wait_bytes(gram_in.at[r], recv_sem.at[gram_phase])
        gram = summed(gram_part[r, rows_of(f), :].astype(F32), gram_in.at[r], GROUP - 1)
        denom = dot_nn(gram.astype(BF16), s_bf[r]) + epsilon
        wait_bytes(numer_in.at[r], recv_sem.at[base_phase])
        numer = summed(numer_part[r, rows_of(f), :].astype(F32), numer_in.at[r], GROUP - 1)
        s_new = s_own[...] * numer / denom
        s_own[...] = s_new
        s_bf[r + 1, rows_of(f), :] = s_new.astype(BF16)
        mine = s_bf.at[r + 1, rows_of(f)]
        for k in frm_steps():
            remote(mine, mine, base_phase + 2, (p, lax.rem(f + k, GROUP))).start()
        wait_bytes(s_bf.at[r + 1, pl.ds(0, COMP - ROWS)], recv_sem.at[base_phase + 2])

        s_now = s_bf[r + 1]
        mixed_part[r, :, pl.ds(0, FRM)] = dot_nt(s_now, norm_t[...]).astype(BF16)
        mixed_part[r, :, pl.ds(FRM, COMP)] = dot_nt(s_now, s_now).astype(BF16)
        half = COMP // 2
        remote(
            mixed_part.at[r, rows_of(1 - c, half)],
            core_in.at[r],
            base_phase + 3,
            (2 * q + 1 - c, f),
        ).start()
        if r == ROUNDS - 1:
            s_out[...] = s_now.astype(F32).T.astype(BF16)
        wait_bytes(core_in.at[r], recv_sem.at[base_phase + 3])
        chip_sum = mixed_part[r, rows_of(c, half), :].astype(F32) + core_in[r].astype(F32)
        chip_part[r] = chip_sum.astype(BF16)
        for slot, k in enumerate(chip_steps()):
            kx, kz = k // 2, k % 2
            x, zh = lax.div(q, 2), lax.rem(q, 2)
            other = lax.rem(x + kx, 4) * 2 + lax.rem(zh + kz, 2)
            remote(
                chip_part.at[r, rows_of(other)],
                chip_in.at[r, slot],
                base_phase + 4,
                (2 * other + c, f),
            ).start()
        wait_bytes(chip_in.at[r], recv_sem.at[base_phase + 4])
        total = summed(chip_part[r, rows_of(q), :].astype(F32), chip_in.at[r], CHIPS - 1)
        denom_t = dot_nn(total[:, FRM:].astype(BF16), t_bf[r]) + epsilon
        t_new = t_own[...] * total[:, :FRM] / denom_t
        t_own[...] = t_new
        t_bf[r + 1, rows_of(comp_block), :] = t_new.astype(BF16)
        own_rows = t_bf.at[r + 1, rows_of(comp_block)]
        for k in sorted(range(1, GROUP), key=lambda k: -(k % 4 // 2)):
            remote(own_rows, own_rows, base_phase + 5, (lax.rem(p + k, GROUP), f)).start()
        wait_bytes(t_bf.at[r + 1, pl.ds(0, COMP - ROWS)], recv_sem.at[base_phase + 5])

    t_out[...] = t_bf[ROUNDS]

    @pl.when(f < GROUP - 1)
    def _():
        to_right.wait_send()

    @pl.when(f > 0)
    def _():
        to_left.wait_send()

    wait_bytes(gram_in.at[0], send_sem.at[0])
    for r in range(ROUNDS):
        base_phase = 1 + 6 * r
        wait_bytes(numer_in.at[r], send_sem.at[base_phase])
        if r:
            wait_bytes(gram_in.at[r], send_sem.at[base_phase + 1])
        wait_bytes(s_bf.at[r + 1, pl.ds(0, COMP - ROWS)], send_sem.at[base_phase + 2])
        wait_bytes(core_in.at[r], send_sem.at[base_phase + 3])
        wait_bytes(chip_in.at[r], send_sem.at[base_phase + 4])
        wait_bytes(t_bf.at[r + 1, pl.ds(0, COMP - ROWS)], send_sem.at[base_phase + 5])


def on_device(movie, taps, scale, base, spatial, temporal):
    phases = 1 + 6 * ROUNDS
    s, t = pl.pallas_call(
        kernel,
        out_shape=(
            jax.ShapeDtypeStruct((PIX, COMP), BF16),
            jax.ShapeDtypeStruct((COMP, FRM), BF16),
        ),
        in_specs=[pl.BlockSpec(memory_space=pl.ANY)] * 6,
        out_specs=(pl.BlockSpec(memory_space=pltpu.VMEM),) * 2,
        scratch_shapes=[
            pltpu.VMEM((PIX, 2 * FRM), BF16),
            pltpu.VMEM((1, TAPS), F32),
            pltpu.VMEM((1, PIX), F32),
            pltpu.VMEM((1, PIX), F32),
            pltpu.VMEM((PIX, COMP), F32),
            pltpu.VMEM((COMP, FRM), F32),
            pltpu.VMEM((1, 2 * FRM), F32),
            pltpu.VMEM((FRM, PIX), BF16),
            pltpu.VMEM((COMP, PIX), F32),
            pltpu.VMEM((ROWS, PIX), F32),
            pltpu.VMEM((ROWS, FRM), F32),
            pltpu.VMEM((ROUNDS + 1, COMP, FRM), BF16),
            pltpu.VMEM((ROUNDS, COMP, COMP), BF16),
            pltpu.VMEM((ROUNDS, COMP, PIX), BF16),
            pltpu.VMEM((ROUNDS, GROUP - 1, ROWS, COMP), BF16),
            pltpu.VMEM((ROUNDS, GROUP - 1, ROWS, PIX), BF16),
            pltpu.VMEM((ROUNDS + 1, COMP, PIX), BF16),
            pltpu.VMEM((ROUNDS, COMP, FRM + COMP), BF16),
            pltpu.VMEM((ROUNDS, COMP // 2, FRM + COMP), BF16),
            pltpu.VMEM((ROUNDS, COMP // 2, FRM + COMP), BF16),
            pltpu.VMEM((ROUNDS, CHIPS - 1, ROWS, FRM + COMP), BF16),
            pltpu.SemaphoreType.DMA((6,)),
            pltpu.SemaphoreType.DMA((2,)),
            pltpu.SemaphoreType.DMA((2,)),
            pltpu.SemaphoreType.DMA((phases,)),
            pltpu.SemaphoreType.DMA((phases,)),
        ],
        compiler_params=pltpu.CompilerParams(
            collective_id=0, has_side_effects=True, vmem_limit_bytes=32 << 20
        ),
    )(movie, taps[None], scale[None], base[None], spatial, temporal)
    return s.astype(F32), t.astype(F32)


def solution(mesh):
    placed = (P("pix", "frm"), P(), P("pix"), P("pix"), P("pix", None), P(None, "frm"))
    return jax.shard_map(
        on_device,
        mesh=mesh,
        in_specs=placed,
        out_specs=(P("pix", None), P(None, "frm")),
        check_vma=False,
    )
```

time: 229 us -> 87.3 us (0.38)
  the two profiles are of different devices: /device:TPU:33 before, /device:TPU:1 now
where the time goes in v1:
time: 87.3 us; the launch traced here: 87 us
  Pallas kernels  80.6 us (92%)
  local copies, waits for them, and re-layouts  4.29 us (5%)
  other arithmetic  1.55 us (2%)
    pallas_call x1, Pallas kernels, on_device(): pl.pallas_call(kernel, out_shape=(jax.ShapeDtypeStruct((PIX, COMP), BF16)...  80.6 us
    unnamed x12, local copies, waits for them, and re-layouts  4.28 us

profile of v1, /device:TPU:1, one launch (start us, length us, event | category | flops | bytes accessed | tf_op | source)
XLA Modules:
  0.0 87.0 jit_solution(1952290610553932839)
XLA Ops:
  0.6 0.0 copy-start.5
  0.6 0.0 copy-start.4
  0.7 0.7 copy-done.5
  1.3 0.0 copy-start.3
  1.3 0.0 copy-done.4
  1.3 0.7 copy-done.3
  2.0 0.0 copy-start
  2.0 1.0 %copy-done = f32[512,256]{1,0:T(8,128)S(1)} copy-done((f32[512,256]{1,0:T(8,128)S(1)}, f32[512,256]{1,0:T(8,128)}, u32[]{:S(2)}) %copy-start) | copy-done | bytes 524312
  3.0 0.0 copy-start.1
  3.0 0.9 %copy-done.1 = bf16[512,256]{1,0:T(8,128)(2,1)S(1)} copy-done((bf16[512,256]{1,0:T(8,128)(2,1)S(1)}, bf16[512,256]{1,0:T(8,128)(2,1)}, u32[]{:S(2)}) %copy-start.1) | copy-done | bytes 262168
  4.0 0.0 copy-start.2
  4.0 0.9 %copy-done.2 = f32[256,256]{1,0:T(8,128)S(1)} copy-done((f32[256,256]{1,0:T(8,128)S(1)}, f32[256,256]{1,0:T(8,128)}, u32[]{:S(2)}) %copy-start.2) | copy-done | bytes 262168
  4.9 80.6 %shard_map.77 = (bf16[512,256]{1,0:T(8,128)(2,1)S(1)}, bf16[256,256]{1,0:T(8,128)(2,1)S(1)}) custom-call(bf16[512,256]{1,0:T(8,128)(2,1)S(1)} %copy-done.1, f32[1,257]{1,0:T(1,128)S(1)} %broadcast_in_dim.9.taps_hbm, f32[1,512]{1,0:T(1,128)S(1)} %bitcast.2, f32[1,512]{1,0:T(1,128)S(1)} %bitcast.3, f32[512,256]{1,0:T(8,128)S(1)} %copy-done, ...), custom_call_target="tpu_custom_call" | custom-call | tf_op jit(solution)/shard_map/pallas_call | solution.py:257
  85.5 0.8 convert_element_type.6
  86.3 0.7 convert_element_type.7
  (1 shorter events, 0.0 us)
Async XLA Ops:
  0.6 0.7 copy-start.5
  0.6 0.7 copy-start.4
  1.3 0.7 copy-start.3
  2.0 1.0 %copy-start = (f32[512,256]{1,0:T(8,128)S(1)}, f32[512,256]{1,0:T(8,128)}, u32[]{:S(2)}) copy-start(f32[512,256]{1,0:T(8,128)} %spatial_hbm.1) | copy-start | bytes 1572868
  3.0 0.9 %copy-start.1 = (bf16[512,256]{1,0:T(8,128)(2,1)S(1)}, bf16[512,256]{1,0:T(8,128)(2,1)}, u32[]{:S(2)}) copy-start(bf16[512,256]{1,0:T(8,128)(2,1)} %movie_hbm.1) | copy-start | bytes 786436
  4.0 0.9 %copy-start.2 = (f32[256,256]{1,0:T(8,128)S(1)}, f32[256,256]{1,0:T(8,128)}, u32[]{:S(2)}) copy-start(f32[256,256]{1,0:T(8,128)} %temporal_hbm.1) | copy-start | bytes 786436

commit v2 on v1

--- a/solution.py
+++ b/solution.py
@@ -37,6 +37,16 @@
 
 def dot_nt(a, b):
     return lax.dot_general(a, b, (((1,), (1,)), ((), ())), preferred_element_type=F32)
+
+
+def product(gram, whole, block, own, own_copy):
+    high = gram.astype(BF16)
+    low = (gram - high.astype(F32)).astype(BF16)
+    both = dot_nn(jnp.concatenate([high, low], axis=0), whole)
+    row = lax.broadcasted_iota(jnp.int32, gram.shape, 0)
+    column = lax.broadcasted_iota(jnp.int32, gram.shape, 1)
+    diagonal = jnp.sum(jnp.where(column == row + block * ROWS, gram, 0.0), axis=1, keepdims=True)
+    return both[:ROWS] + both[ROWS:] + diagonal * (own - own_copy.astype(F32))
 
 
 def rows_of(index, count=ROWS):
@@ -151,7 +161,7 @@
         copy.wait()
     coef[...] = jnp.zeros_like(coef)
     centre = lax.broadcasted_iota(jnp.int32, (1, TAPS), 1) == HALO
-    coef[:, pl.ds(0, TAPS)] = jnp.where(centre, 1.0, 0.0).astype(F32) - taps_v[...]
+    coef[:, pl.ds(0, TAPS)] = jnp.where(centre, 1.0, 0.0).astype(F32) - taps_v[...][None]
     band_t = pltpu.roll(
         jnp.broadcast_to(coef[...], (FRM, 2 * FRM)), 0, 1, stride=1, stride_axis=0
     ).astype(BF16)
@@ -171,7 +181,7 @@
         to_left.wait_recv()
 
     mixed = dot_nt(band_t, padded[...])
-    norm_t[...] = jnp.maximum(scale_v[...] * mixed + base_v[...], 0.0).astype(BF16)
+    norm_t[...] = jnp.maximum(scale_v[...][None] * mixed + base_v[...][None], 0.0).astype(BF16)
 
     for r in range(ROUNDS):
         base_phase = 1 + 6 * r
@@ -183,7 +193,7 @@
         gram_phase = base_phase + 1 if r else 0
         wait_bytes(gram_in.at[r], recv_sem.at[gram_phase])
         gram = summed(gram_part[r, rows_of(f), :].astype(F32), gram_in.at[r], GROUP - 1)
-        denom = dot_nn(gram.astype(BF16), s_bf[r]) + epsilon
+        denom = product(gram, s_bf[r], f, s_own[...], s_bf[r, rows_of(f), :]) + epsilon
         wait_bytes(numer_in.at[r], recv_sem.at[base_phase])
         numer = summed(numer_part[r, rows_of(f), :].astype(F32), numer_in.at[r], GROUP - 1)
         s_new = s_own[...] * numer / denom
@@ -221,7 +231,9 @@
             ).start()
         wait_bytes(chip_in.at[r], recv_sem.at[base_phase + 4])
         total = summed(chip_part[r, rows_of(q), :].astype(F32), chip_in.at[r], CHIPS - 1)
-        denom_t = dot_nn(total[:, FRM:].astype(BF16), t_bf[r]) + epsilon
+        gram_t = total[:, FRM:]
+        t_copy = t_bf[r, rows_of(comp_block), :]
+        denom_t = product(gram_t, t_bf[r], comp_block, t_own[...], t_copy) + epsilon
         t_new = t_own[...] * total[:, :FRM] / denom_t
         t_own[...] = t_new
         t_bf[r + 1, rows_of(comp_block), :] = t_new.astype(BF16)
@@ -252,6 +264,25 @@
         wait_bytes(t_bf.at[r + 1, pl.ds(0, COMP - ROWS)], send_sem.at[base_phase + 5])
 
 
+def widen(s_hbm, t_hbm, s_out, t_out, s_v, t_v, s_w, t_w, sem):
+    into = [
+        pltpu.make_async_copy(t_hbm, t_v, sem.at[0]),
+        pltpu.make_async_copy(s_hbm, s_v, sem.at[1]),
+    ]
+    out = [
+        pltpu.make_async_copy(t_w, t_out, sem.at[2]),
+        pltpu.make_async_copy(s_w, s_out, sem.at[3]),
+    ]
+    for copy in into:
+        copy.start()
+    for narrow, wide, copy, back in zip((t_v, s_v), (t_w, s_w), into, out):
+        copy.wait()
+        wide[...] = narrow[...].astype(F32)
+        back.start()
+    for back in out:
+        back.wait()
+
+
 def on_device(movie, taps, scale, base, spatial, temporal):
     phases = 1 + 6 * ROUNDS
     s, t = pl.pallas_call(
@@ -260,13 +291,13 @@
             jax.ShapeDtypeStruct((PIX, COMP), BF16),
             jax.ShapeDtypeStruct((COMP, FRM), BF16),
         ),
-        in_specs=[pl.BlockSpec(memory_space=pl.ANY)] * 6,
+        in_specs=[pl.BlockSpec(memory_space=pltpu.HBM)] * 6,
         out_specs=(pl.BlockSpec(memory_space=pltpu.VMEM),) * 2,
         scratch_shapes=[
             pltpu.VMEM((PIX, 2 * FRM), BF16),
-            pltpu.VMEM((1, TAPS), F32),
-            pltpu.VMEM((1, PIX), F32),
-            pltpu.VMEM((1, PIX), F32),
+            pltpu.VMEM((TAPS,), F32),
+            pltpu.VMEM((PIX,), F32),
+            pltpu.VMEM((PIX,), F32),
             pltpu.VMEM((PIX, COMP), F32),
             pltpu.VMEM((COMP, FRM), F32),
             pltpu.VMEM((1, 2 * FRM), F32),
@@ -291,10 +322,26 @@
             pltpu.SemaphoreType.DMA((phases,)),
         ],
         compiler_params=pltpu.CompilerParams(
-            collective_id=0, has_side_effects=True, vmem_limit_bytes=32 << 20
+            collective_id=0, has_side_effects=True, vmem_limit_bytes=60 << 20
         ),
-    )(movie, taps[None], scale[None], base[None], spatial, temporal)
-    return s.astype(F32), t.astype(F32)
+    )(movie, taps, scale, base, spatial, temporal)
+    return pl.pallas_call(
+        widen,
+        out_shape=(
+            jax.ShapeDtypeStruct((PIX, COMP), F32),
+            jax.ShapeDtypeStruct((COMP, FRM), F32),
+        ),
+        in_specs=[pl.BlockSpec(memory_space=pltpu.HBM)] * 2,
+        out_specs=(pl.BlockSpec(memory_space=pltpu.HBM),) * 2,
+        scratch_shapes=[
+            pltpu.VMEM((PIX, COMP), BF16),
+            pltpu.VMEM((COMP, FRM), BF16),
+            pltpu.VMEM((PIX, COMP), F32),
+            pltpu.VMEM((COMP, FRM), F32),
+            pltpu.SemaphoreType.DMA((4,)),
+        ],
+        compiler_params=pltpu.CompilerParams(vmem_limit_bytes=60 << 20),
+    )(s, t)
 
 
 def solution(mesh):

time: 87.3 us -> 84.1 us (0.963)
  local copies, waits for them, and re-layouts: 4.29 us -> 0 us
  Pallas kernels: 80.6 us -> 83.4 us
  other arithmetic: 1.55 us -> 0 us
    unnamed x12 -> x0, local copies, waits for them, and re-layouts: 4.28 us -> none
    pallas_call x0 -> x1, Pallas kernels: none -> 1.88 us  [on_device(): pl.pallas_call(widen, out_shape=(jax.ShapeDtypeStruct((PIX, COMP), F32),...]
    convert_element_type x2 -> x0, other arithmetic: 1.55 us -> none  [on_device(): return (s.astype(F32), t.astype(F32))]
    pallas_call x1, Pallas kernels: 80.6 us -> 81.5 us  [on_device(): pl.pallas_call(kernel, out_shape=(jax.ShapeDtypeStruct((PIX, COMP), BF16)...]
where the time goes in v2:
time: 84.1 us; the launch traced here: 84 us
  Pallas kernels  83.4 us (99%)
    pallas_call x1, Pallas kernels, on_device(): pl.pallas_call(kernel, out_shape=(jax.ShapeDtypeStruct((PIX, COMP), BF16)...  81.5 us
    pallas_call x1, Pallas kernels, on_device(): pl.pallas_call(widen, out_shape=(jax.ShapeDtypeStruct((PIX, COMP), F32),...  1.88 us

profile of v2, /device:TPU:1, one launch (start us, length us, event | category | flops | bytes accessed | tf_op | source)
XLA Modules:
  0.0 84.0 jit_solution(10497756029298629908)
XLA Ops:
  0.6 81.5 %shard_map.77 = (bf16[512,256]{1,0:T(8,128)(2,1)}, bf16[256,256]{1,0:T(8,128)(2,1)}) custom-call(bf16[512,256]{1,0:T(8,128)(2,1)} %movie_hbm.1, f32[257]{0:T(512)} %taps_hbm.1, f32[512]{0:T(512)} %scale_hbm.1, f32[512]{0:T(512)} %base_hbm.1, f32[512,256]{1,0:T(8,128)} %spatial_hbm.1, f32[256,256]{1,0:T(8,128)} %temporal_hbm.1), custom_call_target="tpu_custom_call" | custom-call | tf_op jit(solution)/shard_map/pallas_call | solution.py:288
  82.1 1.9 %shard_map.78 = (f32[512,256]{1,0:T(8,128)}, f32[256,256]{1,0:T(8,128)}) custom-call(bf16[512,256]{1,0:T(8,128)(2,1)} %get-tuple-element.4.s_hbm, bf16[256,256]{1,0:T(8,128)(2,1)} %get-tuple-element.5.t_hbm), custom_call_target="tpu_custom_call" | custom-call | tf_op jit(solution)/shard_map/pallas_call | solution.py:328

commit v3 on v1

v3 whole, which is shorter than its diff:
```python
import functools

import jax
import jax.numpy as jnp
from jax import lax
from jax.experimental import pallas as pl
from jax.experimental.pallas import tpu as pltpu
from jax.sharding import PartitionSpec as P

ROUNDS = 2
MESH = pl.DeviceIdType.MESH
F32 = jnp.float32
BF16 = jnp.bfloat16
epsilon = 1e-06

GROUP = 16
CHIPS = 8
PIX = 512
FRM = 256
COMP = 256
ROWS = COMP // GROUP
HALO = 128
SPLIT = 2
PART = PIX // SPLIT
HALF = COMP // 2
TAPS = 257


def far_first(steps, hops):
    return sorted(steps, key=lambda step: -hops(*step))


FRM_STEPS = far_first(
    [(dzl, dy) for dzl in range(4) for dy in range(4) if dzl or dy],
    lambda dzl, dy: dzl + min(dy, 4 - dy),
)
CHIP_STEPS = far_first(
    [(dx, dzh) for dx in range(4) for dzh in range(2) if dx or dzh],
    lambda dx, dzh: min(dx, 4 - dx) + 4 * dzh,
)
PIX_STEPS = far_first(
    [(dx, dzh, dc) for dx in range(4) for dzh in range(2) for dc in range(2) if dx or dzh or dc],
    lambda dx, dzh, dc: min(dx, 4 - dx) + 4 * dzh + 0.5 * dc,
)


def dot_nn(a, b):
    return lax.dot_general(a, b, (((1,), (0,)), ((), ())), preferred_element_type=F32)


def dot_nt(a, b):
    return lax.dot_general(a, b, (((1,), (1,)), ((), ())), preferred_element_type=F32)


def split(value):
    high = value.astype(BF16)
    return high, (value - high.astype(F32)).astype(BF16)


def product(gram, wholes, block, owns, own_copies):
    terms = jnp.concatenate(split(gram), axis=0)
    row = lax.broadcasted_iota(jnp.int32, gram.shape, 0)
    column = lax.broadcasted_iota(jnp.int32, gram.shape, 1)
    diagonal = jnp.sum(jnp.where(column == row + block * ROWS, gram, 0.0), axis=1, keepdims=True)
    results = []
    for whole, own, copy in zip(wholes, owns, own_copies):
        both = dot_nn(terms, whole)
        results.append(both[:ROWS] + both[ROWS:] + diagonal * (own - copy.astype(F32)))
    return results


def rows_of(index, count=ROWS):
    return pl.ds(pl.multiple_of(index * count, count), count)


def wait_bytes(ref, sem):
    pltpu.make_async_copy(ref, ref, sem).wait()


def summed(inbox, count):
    total = inbox[0].astype(F32)
    for slot in range(1, count):
        total = total + inbox[slot].astype(F32)
    return total


NUMER, GRAM, SHARE, LOW, CORE_GRAM, CORE, CHIP, NEAR, FAR, RELAY = 0, 2, 3, 5, 7, 8, 9, 10, 11, 12
PHASES = 14


def kernel(
    movie_hbm, taps_hbm, scale_hbm, base_hbm, spatial_hbm, temporal_hbm,
    s_out, t_out,
    padded, taps_v, scale_v, base_v, spatial_v, temporal_v,
    coef, norm_t, s_zero_t, s_own, t_own, t_bf,
    gram_part, gram_in, gram_own, numer_part, numer_in, s_bf, s_low,
    mixed_part, core_in, chip_part, chip_in, s_wide, t_wide,
    load_sem, halo_send, halo_recv, send_sem, recv_sem, out_sem,
):
    p = lax.axis_index("pix")
    f = lax.axis_index("frm")
    x, zh, c = lax.div(p, 4), lax.rem(lax.div(p, 2), 2), lax.rem(p, 2)
    zl, y = lax.div(f, 4), lax.rem(f, 4)
    pix_block = zh * 4 + x
    t_block = c * CHIPS + pix_block

    def pix_at(dx, dzh, dc):
        return lax.rem(x + dx, 4), lax.rem(zh + dzh, 2), lax.rem(c + dc, 2)

    def pix_device(ox, ozh, oc):
        return ((ox * 2 + ozh) * 2 + oc, f)

    def frm_at(dzl, dy):
        return lax.rem(zl + dzl, 4) * 4 + lax.rem(y + dy, 4)

    barrier = pltpu.get_barrier_semaphore()
    for k in range(1, GROUP):
        pl.semaphore_signal(
            barrier, inc=1, device_id=(lax.rem(p + k, GROUP), f), device_id_type=MESH
        )
        pl.semaphore_signal(
            barrier, inc=1, device_id=(p, lax.rem(f + k, GROUP)), device_id_type=MESH
        )

    loads = [
        pltpu.make_async_copy(src, dst, load_sem.at[i])
        for i, (src, dst) in enumerate(
            (
                (movie_hbm, padded.at[:, pl.ds(HALO, FRM)]),
                (temporal_hbm, temporal_v),
                (spatial_hbm, spatial_v),
                (taps_hbm, taps_v),
                (scale_hbm, scale_v),
                (base_hbm, base_v),
            )
        )
    ]
    for copy in loads:
        copy.start()

    def remote(src, dst, sem, target):
        return pltpu.make_async_remote_copy(
            src_ref=src,
            dst_ref=dst,
            send_sem=send_sem.at[sem],
            recv_sem=recv_sem.at[sem],
            device_id=target,
            device_id_type=MESH,
        )

    pl.semaphore_wait(barrier, 2 * (GROUP - 1))
    loads[0].wait()
    halos = []
    for h in range(SPLIT):
        pixels = pl.ds(h * PART, PART)
        for side, (source, target, step) in enumerate(
            ((FRM, 0, 1), (HALO, HALO + FRM, GROUP - 1))
        ):
            halos.append(
                pltpu.make_async_remote_copy(
                    src_ref=padded.at[pixels, pl.ds(source, HALO)],
                    dst_ref=padded.at[pixels, pl.ds(target, HALO)],
                    send_sem=halo_send.at[2 * h + side],
                    recv_sem=halo_recv.at[2 * h + side],
                    device_id=(p, lax.rem(f + step, GROUP)),
                    device_id_type=MESH,
                )
            )
    has_right, has_left = f < GROUP - 1, f > 0

    @pl.when(has_right)
    def _():
        for copy in halos[0::2]:
            copy.start()

    @pl.when(has_left)
    def _():
        for copy in halos[1::2]:
            copy.start()

    def send_gram(r):
        t_now = t_bf[r]
        t_half = t_bf[r, rows_of(c, HALF), :]
        gram_part[r] = dot_nt(t_now, t_half).astype(BF16)
        for dzl, dy in FRM_STEPS:
            other = frm_at(dzl, dy)
            remote(
                gram_part.at[r, rows_of(other)], gram_in.at[r, f], r * PHASES + GRAM, (p, other)
            ).start()
        gram_in[r, f] = gram_part[r, rows_of(f), :]

    def finish_gram(r):
        wait_bytes(gram_in.at[r, pl.ds(0, GROUP - 1)], recv_sem.at[r * PHASES + GRAM])
        half = pl.ds(pl.multiple_of(c * HALF, HALF), HALF)
        gram_own[r, :, half] = summed(gram_in.at[r], GROUP)
        mine = gram_own.at[r, :, half]
        copy = remote(mine, mine, r * PHASES + CORE_GRAM, pix_device(x, zh, 1 - c))
        copy.start()
        copy.wait_recv()

    loads[1].wait()
    t_bf[0] = temporal_v[...].astype(BF16)
    send_gram(0)

    @pl.when(f == 0)
    def _():
        padded[:, pl.ds(0, HALO)] = jnp.zeros((PIX, HALO), BF16)

    @pl.when(f == GROUP - 1)
    def _():
        padded[:, pl.ds(HALO + FRM, HALO)] = jnp.zeros((PIX, HALO), BF16)

    for copy in loads[2:]:
        copy.wait()
    coef[...] = jnp.zeros_like(coef)
    centre = lax.broadcasted_iota(jnp.int32, (1, TAPS), 1) == HALO
    coef[:, pl.ds(0, TAPS)] = jnp.where(centre, 1.0, 0.0).astype(F32) - taps_v[...][None]
    band_t = pltpu.roll(
        jnp.broadcast_to(coef[...], (FRM, 2 * FRM)), 0, 1, stride=1, stride_axis=0
    ).astype(BF16)
    spatial_t = spatial_v[...].T
    for h in range(SPLIT):
        s_zero_t[h] = spatial_t[:, h * PART : (h + 1) * PART]
        s_bf[0, h] = s_zero_t[h].astype(BF16)
        s_own[h] = s_zero_t[h, rows_of(f), :]
    t_own[...] = temporal_v[rows_of(t_block), :]

    def send_numer(r, h, others):
        for other in others:
            remote(
                numer_part.at[r, h, rows_of(other)],
                numer_in.at[r, h, f],
                r * PHASES + NUMER + h,
                (p, other),
            ).start()

    for h in range(SPLIT):
        pixels = pl.ds(h * PART, PART)

        @pl.when(has_left)
        def _():
            halos[2 * h].wait_recv()

        @pl.when(has_right)
        def _():
            halos[2 * h + 1].wait_recv()

        mixed = dot_nt(band_t, padded[pixels, :])
        scaled = scale_v[pixels][None] * mixed + base_v[pixels][None]
        norm_t[h] = jnp.maximum(scaled, 0.0).astype(BF16)
        numer_part[0, h] = dot_nn(t_bf[0], norm_t[h]).astype(BF16)
        send_numer(0, h, [frm_at(dzl, dy) for dzl, dy in FRM_STEPS])
        numer_in[0, h, f] = numer_part[0, h, rows_of(f), :]

    for r in range(ROUNDS):
        last = r == ROUNDS - 1
        at = r * PHASES
        finish_gram(r)
        denoms = product(
            gram_own[r],
            [s_bf[r, h] for h in range(SPLIT)],
            f,
            [s_own[h] for h in range(SPLIT)],
            [s_bf[r, h, rows_of(f), :] for h in range(SPLIT)],
        )
        for h in range(SPLIT):
            wait_bytes(numer_in.at[r, h, pl.ds(0, GROUP - 1)], recv_sem.at[at + NUMER + h])
            numer = summed(numer_in.at[r, h], GROUP)
            s_new = s_own[h] * numer / (denoms[h] + epsilon)
            s_own[h] = s_new
            high, low = split(s_new)
            s_bf[r + 1, h, rows_of(f), :] = high
            mine = s_bf.at[r + 1, h, rows_of(f)]
            for dzl, dy in FRM_STEPS:
                remote(mine, mine, at + SHARE + h, (p, frm_at(dzl, dy))).start()
            if last:
                s_low[h, rows_of(f), :] = low
        if last:
            for h in range(SPLIT):
                mine = s_low.at[h, rows_of(f)]
                for dzl, dy in FRM_STEPS:
                    remote(mine, mine, at + LOW + h, (p, frm_at(dzl, dy))).start()

        numer_t = gram_t = 0.0
        for h in range(SPLIT):
            wait_bytes(s_bf.at[r + 1, h, pl.ds(0, COMP - ROWS)], recv_sem.at[at + SHARE + h])
            s_now = s_bf[r + 1, h]
            numer_t = numer_t + dot_nt(s_now, norm_t[h])
            gram_t = gram_t + dot_nt(s_now, s_now)
        mixed_part[r, :, pl.ds(0, FRM)] = numer_t.astype(BF16)
        mixed_part[r, :, pl.ds(FRM, COMP)] = gram_t.astype(BF16)
        remote(
            mixed_part.at[r, rows_of(1 - c, HALF)],
            core_in.at[r],
            at + CORE,
            pix_device(x, zh, 1 - c),
        ).start()
        wait_bytes(core_in.at[r], recv_sem.at[at + CORE])
        chip_sum = mixed_part[r, rows_of(c, HALF), :].astype(F32) + core_in[r].astype(F32)
        chip_part[r] = chip_sum.astype(BF16)
        for dx, dzh in CHIP_STEPS:
            ox, ozh, _ = pix_at(dx, dzh, 0)
            remote(
                chip_part.at[r, rows_of(ozh * 4 + ox)],
                chip_in.at[r, pix_block],
                at + CHIP,
                pix_device(ox, ozh, c),
            ).start()
        chip_in[r, pix_block] = chip_part[r, rows_of(pix_block), :]
        if last:
            for h in range(SPLIT):
                wait_bytes(s_low.at[h, pl.ds(0, COMP - ROWS)], recv_sem.at[at + LOW + h])
                whole = s_bf[r + 1, h].astype(F32) + s_low[h].astype(F32)
                s_wide[pl.ds(h * PART, PART), :] = whole.T
            pltpu.make_async_copy(s_wide, s_out, out_sem.at[0]).start()
        wait_bytes(chip_in.at[r, pl.ds(0, CHIPS - 1)], recv_sem.at[at + CHIP])
        total = summed(chip_in.at[r], CHIPS)
        (denom_t,) = product(
            total[:, FRM:], [t_bf[r]], t_block, [t_own[...]], [t_bf[r, rows_of(t_block), :]]
        )
        t_new = t_own[...] * total[:, :FRM] / (denom_t + epsilon)
        t_own[...] = t_new
        if not last:
            t_bf[r + 1, rows_of(t_block), :] = t_new.astype(BF16)
            mine = t_bf.at[r + 1, rows_of(t_block)]
            for dx, dzh, dc in PIX_STEPS:
                sem = at + (FAR if dzh else NEAR)
                remote(mine, mine, sem, pix_device(*pix_at(dx, dzh, dc))).start()
            for part, sem, count in ((0, NEAR, CHIPS - 1), (1, FAR, CHIPS)):
                wait_bytes(t_bf.at[r + 1, pl.ds(0, count * ROWS)], recv_sem.at[at + sem])
                if part:
                    send_gram(r + 1)
                group = lax.rem(zh + part, 2)
                spans = [pl.ds(pl.multiple_of(b * HALF + group * 64, 64), 64) for b in range(2)]
                t_rows = jnp.concatenate([t_bf[r + 1, span, :] for span in spans], axis=0)
                first = lax.rem(zl + group, 2)
                for h in range(SPLIT):
                    rows = dot_nn(t_rows, norm_t[h]).astype(BF16)
                    for b, span in enumerate(spans):
                        numer_part[r + 1, h, span, :] = rows[b * 64 : (b + 1) * 64]
                for h in range(SPLIT):
                    for i in (2, 0):
                        for dy in (2, 1, 3, 0):
                            other = frm_at(first + i, dy)
                            if i or dy:
                                send_numer(r + 1, h, [other])
                            else:

                                @pl.when(first > 0)
                                def _():
                                    send_numer(r + 1, h, [other])

            for h in range(SPLIT):
                numer_in[r + 1, h, f] = numer_part[r + 1, h, rows_of(f), :]
        else:
            t_wide[rows_of(t_block), :] = t_new
            mine = t_wide.at[rows_of(t_block)]
            for dx, dzh in CHIP_STEPS:
                ox, ozh, _ = pix_at(dx, dzh, 0)
                sem = at + (FAR if dzh else NEAR)
                remote(mine, mine, sem, pix_device(ox, ozh, c)).start()
            for part, sem, count in ((0, NEAR, 3), (1, FAR, 4)):
                wait_bytes(t_wide.at[pl.ds(0, count * ROWS)], recv_sem.at[at + sem])
                group = lax.rem(zh + part, 2)
                got = t_wide.at[pl.ds(pl.multiple_of(c * HALF + group * 64, 64), 64)]
                remote(got, got, at + RELAY + part, pix_device(x, zh, 1 - c)).start()
            for part in range(2):
                wait_bytes(t_wide.at[pl.ds(0, 64)], recv_sem.at[at + RELAY + part])
    result = pltpu.make_async_copy(t_wide, t_out, out_sem.at[1])
    result.start()

    @pl.when(has_right)
    def _():
        for copy in halos[0::2]:
            copy.wait_send()

    @pl.when(has_left)
    def _():
        for copy in halos[1::2]:
            copy.wait_send()

    for r in range(ROUNDS):
        last = r == ROUNDS - 1
        at = r * PHASES
        sent = [
            (GRAM, gram_in.at[r, pl.ds(0, GROUP - 1)]),
            (CORE_GRAM, gram_own.at[r, :, pl.ds(0, HALF)]),
            (CORE, core_in.at[r]),
            (CHIP, chip_in.at[r, pl.ds(0, CHIPS - 1)]),
        ]
        for h in range(SPLIT):
            sent.append((NUMER + h, numer_in.at[r, h, pl.ds(0, GROUP - 1)]))
            sent.append((SHARE + h, s_bf.at[r + 1, h, pl.ds(0, COMP - ROWS)]))
        if last:
            sent += [(LOW + h, s_low.at[h, pl.ds(0, COMP - ROWS)]) for h in range(SPLIT)]
            sent += [(NEAR, t_wide.at[pl.ds(0, 3 * ROWS)]), (FAR, t_wide.at[pl.ds(0, 4 * ROWS)])]
            sent += [(RELAY + part, t_wide.at[pl.ds(0, 64)]) for part in range(2)]
        else:
            sent += [
                (NEAR, t_bf.at[r + 1, pl.ds(0, 7 * ROWS)]),
                (FAR, t_bf.at[r + 1, pl.ds(0, 8 * ROWS)]),
            ]
        for sem, ref in sent:
            wait_bytes(ref, send_sem.at[at + sem])
    pltpu.make_async_copy(s_wide, s_out, out_sem.at[0]).wait()
    result.wait()


def hand_on(s_hbm, t_hbm, s_out, t_out, sem):
    copies = [
        pltpu.make_async_copy(s_hbm, s_out, sem.at[0]),
        pltpu.make_async_copy(t_hbm, t_out, sem.at[1]),
    ]
    for copy in copies:
        copy.start()
    for copy in copies:
        copy.wait()


def on_device(movie, taps, scale, base, spatial, temporal):
    hbm = pl.BlockSpec(memory_space=pltpu.HBM)
    shapes = (
        jax.ShapeDtypeStruct((PIX, COMP), F32),
        jax.ShapeDtypeStruct((COMP, FRM), F32),
    )
    s, t = pl.pallas_call(
        kernel,
        out_shape=shapes,
        in_specs=[hbm] * 6,
        out_specs=(hbm, hbm),
        scratch_shapes=[
            pltpu.VMEM((PIX, 2 * FRM), BF16),
            pltpu.VMEM((TAPS,), F32),
            pltpu.VMEM((PIX,), F32),
            pltpu.VMEM((PIX,), F32),
            pltpu.VMEM((PIX, COMP), F32),
            pltpu.VMEM((COMP, FRM), F32),
            pltpu.VMEM((1, 2 * FRM), F32),
            pltpu.VMEM((SPLIT, FRM, PART), BF16),
            pltpu.VMEM((SPLIT, COMP, PART), F32),
            pltpu.VMEM((SPLIT, ROWS, PART), F32),
            pltpu.VMEM((ROWS, FRM), F32),
            pltpu.VMEM((ROUNDS, COMP, FRM), BF16),
            pltpu.VMEM((ROUNDS, COMP, HALF), BF16),
            pltpu.VMEM((ROUNDS, GROUP, ROWS, HALF), BF16),
            pltpu.VMEM((ROUNDS, ROWS, COMP), F32),
            pltpu.VMEM((ROUNDS, SPLIT, COMP, PART), BF16),
            pltpu.VMEM((ROUNDS, SPLIT, GROUP, ROWS, PART), BF16),
            pltpu.VMEM((ROUNDS + 1, SPLIT, COMP, PART), BF16),
            pltpu.VMEM((SPLIT, COMP, PART), BF16),
            pltpu.VMEM((ROUNDS, COMP, FRM + COMP), BF16),
            pltpu.VMEM((ROUNDS, HALF, FRM + COMP), BF16),
            pltpu.VMEM((ROUNDS, HALF, FRM + COMP), BF16),
            pltpu.VMEM((ROUNDS, CHIPS, ROWS, FRM + COMP), BF16),
            pltpu.VMEM((PIX, COMP), F32),
            pltpu.VMEM((COMP, FRM), F32),
            pltpu.SemaphoreType.DMA((6,)),
            pltpu.SemaphoreType.DMA((2 * SPLIT,)),
            pltpu.SemaphoreType.DMA((2 * SPLIT,)),
            pltpu.SemaphoreType.DMA((ROUNDS * PHASES,)),
            pltpu.SemaphoreType.DMA((ROUNDS * PHASES,)),
            pltpu.SemaphoreType.DMA((2,)),
        ],
        compiler_params=pltpu.CompilerParams(
            collective_id=0, has_side_effects=True, vmem_limit_bytes=60 << 20
        ),
    )(movie, taps, scale, base, spatial, temporal)
    return pl.pallas_call(
        hand_on,
        out_shape=shapes,
        in_specs=[hbm, hbm],
        out_specs=(hbm, hbm),
        scratch_shapes=[pltpu.SemaphoreType.DMA((2,))],
        compiler_params=pltpu.CompilerParams(vmem_limit_bytes=60 << 20),
    )(s, t)


def solution(mesh):
    placed = (P("pix", "frm"), P(), P("pix"), P("pix"), P("pix", None), P(None, "frm"))
    return jax.shard_map(
        on_device,
        mesh=mesh,
        in_specs=placed,
        out_specs=(P("pix", None), P(None, "frm")),
        check_vma=False,
    )
```

time: 87.3 us -> 105 us (1.20)
  Pallas kernels: 80.6 us -> 104 us
  local copies, waits for them, and re-layouts: 4.29 us -> 0 us
  other arithmetic: 1.55 us -> 0 us
    pallas_call x1 -> x2, Pallas kernels: 80.6 us -> 104 us  [the longest x1 79 us: on_device(): pl.pallas_call(kernel, out_shape=shapes, in_specs=[hbm] * 6, out_specs=(h...]
    unnamed x12 -> x0, local copies, waits for them, and re-layouts: 4.28 us -> none
    convert_element_type x2 -> x0, other arithmetic: 1.55 us -> none  [on_device(): return (s.astype(F32), t.astype(F32))]
where the time goes in v3:
time: 105 us
  Pallas kernels  104 us (99%)
    pallas_call x1, Pallas kernels, on_device(): pl.pallas_call(kernel, out_shape=shapes, in_specs=[hbm] * 6, out_specs=(h...  79 us
    pallas_call x1, Pallas kernels, on_device(): pl.pallas_call(hand_on, out_shape=shapes, in_specs=[hbm, hbm], out_specs=...  24.9 us

profile of v3, /device:TPU:1, one launch (start us, length us, event | category | flops | bytes accessed | tf_op | source)
XLA Modules:
  0.0 104.5 jit_solution(4263890360173930259)
XLA Ops:
  0.6 79.0 %shard_map.77 = (f32[512,256]{1,0:T(8,128)}, f32[256,256]{1,0:T(8,128)}) custom-call(bf16[512,256]{1,0:T(8,128)(2,1)} %movie_hbm.1, f32[257]{0:T(512)} %taps_hbm.1, f32[512]{0:T(512)} %scale_hbm.1, f32[512]{0:T(512)} %base_hbm.1, f32[512,256]{1,0:T(8,128)} %spatial_hbm.1, f32[256,256]{1,0:T(8,128)} %temporal_hbm.1), custom_call_target="tpu_custom_call" | custom-call | tf_op jit(solution)/shard_map/pallas_call | solution.py:426
  79.6 24.9 %shard_map.78 = (f32[512,256]{1,0:T(8,128)}, f32[256,256]{1,0:T(8,128)}) custom-call(f32[512,256]{1,0:T(8,128)} %get-tuple-element.4.s_hbm, f32[256,256]{1,0:T(8,128)} %get-tuple-element.5.t_hbm), custom_call_target="tpu_custom_call" | custom-call | tf_op jit(solution)/shard_map/pallas_call | solution.py:468

commit v4 on v3

--- a/solution.py
+++ b/solution.py
@@ -94,8 +94,8 @@
     padded, taps_v, scale_v, base_v, spatial_v, temporal_v,
     coef, norm_t, s_zero_t, s_own, t_own, t_bf,
     gram_part, gram_in, gram_own, numer_part, numer_in, s_bf, s_low,
-    mixed_part, core_in, chip_part, chip_in, s_wide, t_wide,
-    load_sem, halo_send, halo_recv, send_sem, recv_sem, out_sem,
+    mixed_part, core_in, chip_part, chip_in,
+    load_sem, halo_send, halo_recv, send_sem, recv_sem, met,
 ):
     p = lax.axis_index("pix")
     f = lax.axis_index("frm")
@@ -114,13 +114,27 @@
         return lax.rem(zl + dzl, 4) * 4 + lax.rem(y + dy, 4)
 
     barrier = pltpu.get_barrier_semaphore()
-    for k in range(1, GROUP):
-        pl.semaphore_signal(
-            barrier, inc=1, device_id=(lax.rem(p + k, GROUP), f), device_id_type=MESH
-        )
-        pl.semaphore_signal(
-            barrier, inc=1, device_id=(p, lax.rem(f + k, GROUP)), device_id_type=MESH
-        )
+    x_line = [pix_device(*pix_at(dx, 0, 0)) for dx in (2, 1, 3)]
+    z_far, partner = pix_device(x, 1 - zh, c), pix_device(x, zh, 1 - c)
+    z_line = [(p, frm_at(dzl, 0)) for dzl in (3, 2, 1)]
+    y_line = [(p, frm_at(0, dy)) for dy in (2, 1, 3)]
+
+    def signal(sem, targets):
+        for target in targets:
+            pl.semaphore_signal(sem, inc=1, device_id=target, device_id_type=MESH)
+
+    greeted = [z_far, *z_line, *x_line, *y_line, partner]
+    signal(barrier, greeted)
+    corner_right = jnp.logical_and(y == 3, f < GROUP - 1)
+    corner_left = jnp.logical_and(y == 0, f > 0)
+
+    @pl.when(corner_right)
+    def _():
+        signal(barrier, [(p, f + 1)])
+
+    @pl.when(corner_left)
+    def _():
+        signal(barrier, [(p, f - 1)])
 
     loads = [
         pltpu.make_async_copy(src, dst, load_sem.at[i])
@@ -148,7 +162,17 @@
             device_id_type=MESH,
         )
 
-    pl.semaphore_wait(barrier, 2 * (GROUP - 1))
+    cornered = jnp.logical_or(corner_right, corner_left)
+
+    @pl.when(cornered)
+    def _():
+        pl.semaphore_wait(barrier, len(greeted) + 1)
+
+    @pl.when(jnp.logical_not(cornered))
+    def _():
+        pl.semaphore_wait(barrier, len(greeted))
+
+    met_frm, met_pix, met_core = (met.at[i] for i in range(3))
     loads[0].wait()
     halos = []
     for h in range(SPLIT):
@@ -178,10 +202,15 @@
         for copy in halos[1::2]:
             copy.start()
 
-    def send_gram(r):
+    signal(met_frm, z_line)
+    signal(met_pix, [z_far, *x_line, partner])
+
+    def make_gram(r):
         t_now = t_bf[r]
         t_half = t_bf[r, rows_of(c, HALF), :]
         gram_part[r] = dot_nt(t_now, t_half).astype(BF16)
+
+    def send_gram(r):
         for dzl, dy in FRM_STEPS:
             other = frm_at(dzl, dy)
             remote(
@@ -200,6 +229,8 @@
 
     loads[1].wait()
     t_bf[0] = temporal_v[...].astype(BF16)
+    make_gram(0)
+    pl.semaphore_wait(met_frm, len(z_line))
     send_gram(0)
 
     @pl.when(f == 0)
@@ -224,6 +255,8 @@
         s_bf[0, h] = s_zero_t[h].astype(BF16)
         s_own[h] = s_zero_t[h, rows_of(f), :]
     t_own[...] = temporal_v[rows_of(t_block), :]
+    pl.semaphore_wait(met_pix, 2 + len(x_line))
+    signal(met_core, [partner])
 
     def send_numer(r, h, others):
         for other in others:
@@ -275,11 +308,6 @@
                 remote(mine, mine, at + SHARE + h, (p, frm_at(dzl, dy))).start()
             if last:
                 s_low[h, rows_of(f), :] = low
-        if last:
-            for h in range(SPLIT):
-                mine = s_low.at[h, rows_of(f)]
-                for dzl, dy in FRM_STEPS:
-                    remote(mine, mine, at + LOW + h, (p, frm_at(dzl, dy))).start()
 
         numer_t = gram_t = 0.0
         for h in range(SPLIT):
@@ -298,6 +326,8 @@
         wait_bytes(core_in.at[r], recv_sem.at[at + CORE])
         chip_sum = mixed_part[r, rows_of(c, HALF), :].astype(F32) + core_in[r].astype(F32)
         chip_part[r] = chip_sum.astype(BF16)
+        if not r:
+            pl.semaphore_wait(met_core, 1)
         for dx, dzh in CHIP_STEPS:
             ox, ozh, _ = pix_at(dx, dzh, 0)
             remote(
@@ -309,10 +339,9 @@
         chip_in[r, pix_block] = chip_part[r, rows_of(pix_block), :]
         if last:
             for h in range(SPLIT):
-                wait_bytes(s_low.at[h, pl.ds(0, COMP - ROWS)], recv_sem.at[at + LOW + h])
-                whole = s_bf[r + 1, h].astype(F32) + s_low[h].astype(F32)
-                s_wide[pl.ds(h * PART, PART), :] = whole.T
-            pltpu.make_async_copy(s_wide, s_out, out_sem.at[0]).start()
+                mine = s_low.at[h, rows_of(f)]
+                for dzl, dy in FRM_STEPS:
+                    remote(mine, mine, at + LOW + h, (p, frm_at(dzl, dy))).start()
         wait_bytes(chip_in.at[r, pl.ds(0, CHIPS - 1)], recv_sem.at[at + CHIP])
         total = summed(chip_in.at[r], CHIPS)
         (denom_t,) = product(
@@ -329,6 +358,7 @@
             for part, sem, count in ((0, NEAR, CHIPS - 1), (1, FAR, CHIPS)):
                 wait_bytes(t_bf.at[r + 1, pl.ds(0, count * ROWS)], recv_sem.at[at + sem])
                 if part:
+                    make_gram(r + 1)
                     send_gram(r + 1)
                 group = lax.rem(zh + part, 2)
                 spans = [pl.ds(pl.multiple_of(b * HALF + group * 64, 64), 64) for b in range(2)]
@@ -353,21 +383,23 @@
             for h in range(SPLIT):
                 numer_in[r + 1, h, f] = numer_part[r + 1, h, rows_of(f), :]
         else:
-            t_wide[rows_of(t_block), :] = t_new
-            mine = t_wide.at[rows_of(t_block)]
+            t_out[rows_of(t_block), :] = t_new
+            mine = t_out.at[rows_of(t_block)]
             for dx, dzh in CHIP_STEPS:
                 ox, ozh, _ = pix_at(dx, dzh, 0)
                 sem = at + (FAR if dzh else NEAR)
                 remote(mine, mine, sem, pix_device(ox, ozh, c)).start()
+            for h in range(SPLIT):
+                wait_bytes(s_low.at[h, pl.ds(0, COMP - ROWS)], recv_sem.at[at + LOW + h])
+                whole = s_bf[r + 1, h].astype(F32) + s_low[h].astype(F32)
+                s_out[pl.ds(h * PART, PART), :] = whole.T
             for part, sem, count in ((0, NEAR, 3), (1, FAR, 4)):
-                wait_bytes(t_wide.at[pl.ds(0, count * ROWS)], recv_sem.at[at + sem])
+                wait_bytes(t_out.at[pl.ds(0, count * ROWS)], recv_sem.at[at + sem])
                 group = lax.rem(zh + part, 2)
-                got = t_wide.at[pl.ds(pl.multiple_of(c * HALF + group * 64, 64), 64)]
+                got = t_out.at[pl.ds(pl.multiple_of(c * HALF + group * 64, 64), 64)]
                 remote(got, got, at + RELAY + part, pix_device(x, zh, 1 - c)).start()
             for part in range(2):
-                wait_bytes(t_wide.at[pl.ds(0, 64)], recv_sem.at[at + RELAY + part])
-    result = pltpu.make_async_copy(t_wide, t_out, out_sem.at[1])
-    result.start()
+                wait_bytes(t_out.at[pl.ds(0, 64)], recv_sem.at[at + RELAY + part])
 
     @pl.when(has_right)
     def _():
@@ -393,8 +425,8 @@
             sent.append((SHARE + h, s_bf.at[r + 1, h, pl.ds(0, COMP - ROWS)]))
         if last:
             sent += [(LOW + h, s_low.at[h, pl.ds(0, COMP - ROWS)]) for h in range(SPLIT)]
-            sent += [(NEAR, t_wide.at[pl.ds(0, 3 * ROWS)]), (FAR, t_wide.at[pl.ds(0, 4 * ROWS)])]
-            sent += [(RELAY + part, t_wide.at[pl.ds(0, 64)]) for part in range(2)]
+            sent += [(NEAR, t_out.at[pl.ds(0, 3 * ROWS)]), (FAR, t_out.at[pl.ds(0, 4 * ROWS)])]
+            sent += [(RELAY + part, t_out.at[pl.ds(0, 64)]) for part in range(2)]
         else:
             sent += [
                 (NEAR, t_bf.at[r + 1, pl.ds(0, 7 * ROWS)]),
@@ -402,14 +434,12 @@
             ]
         for sem, ref in sent:
             wait_bytes(ref, send_sem.at[at + sem])
-    pltpu.make_async_copy(s_wide, s_out, out_sem.at[0]).wait()
-    result.wait()
-
-
-def hand_on(s_hbm, t_hbm, s_out, t_out, sem):
+
+
+def hand_on(s_v, t_v, s_out, t_out, sem):
     copies = [
-        pltpu.make_async_copy(s_hbm, s_out, sem.at[0]),
-        pltpu.make_async_copy(t_hbm, t_out, sem.at[1]),
+        pltpu.make_async_copy(s_v, s_out, sem.at[0]),
+        pltpu.make_async_copy(t_v, t_out, sem.at[1]),
     ]
     for copy in copies:
         copy.start()
@@ -419,15 +449,20 @@
 
 def on_device(movie, taps, scale, base, spatial, temporal):
     hbm = pl.BlockSpec(memory_space=pltpu.HBM)
+    vmem = pl.BlockSpec(memory_space=pltpu.VMEM)
     shapes = (
         jax.ShapeDtypeStruct((PIX, COMP), F32),
         jax.ShapeDtypeStruct((COMP, FRM), F32),
     )
+    operands = [
+        pltpu.with_memory_space_constraint(array, pltpu.HBM)
+        for array in (movie, taps, scale, base, spatial, temporal)
+    ]
     s, t = pl.pallas_call(
         kernel,
         out_shape=shapes,
         in_specs=[hbm] * 6,
-        out_specs=(hbm, hbm),
+        out_specs=(vmem, vmem),
         scratch_shapes=[
             pltpu.VMEM((PIX, 2 * FRM), BF16),
             pltpu.VMEM((TAPS,), F32),
@@ -452,26 +487,24 @@
             pltpu.VMEM((ROUNDS, HALF, FRM + COMP), BF16),
             pltpu.VMEM((ROUNDS, HALF, FRM + COMP), BF16),
             pltpu.VMEM((ROUNDS, CHIPS, ROWS, FRM + COMP), BF16),
-            pltpu.VMEM((PIX, COMP), F32),
-            pltpu.VMEM((COMP, FRM), F32),
             pltpu.SemaphoreType.DMA((6,)),
             pltpu.SemaphoreType.DMA((2 * SPLIT,)),
             pltpu.SemaphoreType.DMA((2 * SPLIT,)),
             pltpu.SemaphoreType.DMA((ROUNDS * PHASES,)),
             pltpu.SemaphoreType.DMA((ROUNDS * PHASES,)),
-            pltpu.SemaphoreType.DMA((2,)),
+            pltpu.SemaphoreType.REGULAR((3,)),
         ],
         compiler_params=pltpu.CompilerParams(
-            collective_id=0, has_side_effects=True, vmem_limit_bytes=60 << 20
+            collective_id=0, has_side_effects=True, vmem_limit_bytes=40 << 20
         ),
-    )(movie, taps, scale, base, spatial, temporal)
+    )(*operands)
     return pl.pallas_call(
         hand_on,
         out_shape=shapes,
-        in_specs=[hbm, hbm],
+        in_specs=[vmem, vmem],
         out_specs=(hbm, hbm),
         scratch_shapes=[pltpu.SemaphoreType.DMA((2,))],
-        compiler_params=pltpu.CompilerParams(vmem_limit_bytes=60 << 20),
+        compiler_params=pltpu.CompilerParams(vmem_limit_bytes=40 << 20),
     )(s, t)
 
 

time: 105 us -> 78.6 us (0.75)
  Pallas kernels: 104 us -> 77.9 us
    pallas_call x2, Pallas kernels: 104 us -> 77.9 us  [the longest x1 77 us: on_device(): pl.pallas_call(kernel, out_shape=shapes, in_specs=[hbm] * 6, out_specs=(v...]
where the time goes in v4:
time: 78.6 us; the launch traced here: 78.5 us
  Pallas kernels  77.9 us (99%)
    pallas_call x1, Pallas kernels, on_device(): pl.pallas_call(kernel, out_shape=shapes, in_specs=[hbm] * 6, out_specs=(v...  77 us

profile of v4, /device:TPU:1, one launch (start us, length us, event | category | flops | bytes accessed | tf_op | source)
XLA Modules:
  0.0 78.5 jit_solution(9582673199732846188)
XLA Ops:
  0.6 77.0 %shard_map.77 = (f32[512,256]{1,0:T(8,128)S(1)}, f32[256,256]{1,0:T(8,128)S(1)}) custom-call(bf16[512,256]{1,0:T(8,128)(2,1)} %movie_hbm.1, f32[257]{0:T(512)} %taps_hbm.1, f32[512]{0:T(512)} %scale_hbm.1, f32[512]{0:T(512)} %base_hbm.1, f32[512,256]{1,0:T(8,128)} %spatial_hbm.1, f32[256,256]{1,0:T(8,128)} %temporal_hbm.1), custom_call_target="tpu_custom_call" | custom-call | tf_op jit(solution)/shard_map/pallas_call | solution.py:461
  77.6 0.9 %shard_map.78 = (f32[512,256]{1,0:T(8,128)}, f32[256,256]{1,0:T(8,128)}) custom-call(f32[512,256]{1,0:T(8,128)S(1)} %get-tuple-element.4.s_v, f32[256,256]{1,0:T(8,128)S(1)} %get-tuple-element.5.t_v), custom_call_target="tpu_custom_call" | custom-call | tf_op jit(solution)/shard_map/pallas_call | solution.py:501

commit v5 on v4

--- a/solution.py
+++ b/solution.py
@@ -85,14 +85,15 @@
 
 
 NUMER, GRAM, SHARE, LOW, CORE_GRAM, CORE, CHIP, NEAR, FAR, RELAY = 0, 2, 3, 5, 7, 8, 9, 10, 11, 12
-PHASES = 14
+ACROSS = 14
+PHASES = 15
 
 
 def kernel(
     movie_hbm, taps_hbm, scale_hbm, base_hbm, spatial_hbm, temporal_hbm,
     s_out, t_out,
     padded, taps_v, scale_v, base_v, spatial_v, temporal_v,
-    coef, norm_t, s_zero_t, s_own, t_own, t_bf,
+    coef, norm_t, s_zero_t, s_own, t_own, t_across, t_bf, t_turned,
     gram_part, gram_in, gram_own, numer_part, numer_in, s_bf, s_low,
     mixed_part, core_in, chip_part, chip_in,
     load_sem, halo_send, halo_recv, send_sem, recv_sem, met,
@@ -115,7 +116,8 @@
 
     barrier = pltpu.get_barrier_semaphore()
     x_line = [pix_device(*pix_at(dx, 0, 0)) for dx in (2, 1, 3)]
-    z_far, partner = pix_device(x, 1 - zh, c), pix_device(x, zh, 1 - c)
+    partner = pix_device(x, zh, 1 - c)
+    z_two = [(pix_device(x, 1 - zh, c)[0], frm_at(2, 0)), (p, frm_at(2, 0))]
     z_line = [(p, frm_at(dzl, 0)) for dzl in (3, 2, 1)]
     y_line = [(p, frm_at(0, dy)) for dy in (2, 1, 3)]
 
@@ -123,7 +125,7 @@
         for target in targets:
             pl.semaphore_signal(sem, inc=1, device_id=target, device_id_type=MESH)
 
-    greeted = [z_far, *z_line, *x_line, *y_line, partner]
+    greeted = [*z_line, z_two[0], *x_line, *y_line, partner]
     signal(barrier, greeted)
     corner_right = jnp.logical_and(y == 3, f < GROUP - 1)
     corner_left = jnp.logical_and(y == 0, f > 0)
@@ -172,7 +174,7 @@
     def _():
         pl.semaphore_wait(barrier, len(greeted))
 
-    met_frm, met_pix, met_core = (met.at[i] for i in range(3))
+    met_frm, met_two, met_line, met_pix = (met.at[i] for i in range(4))
     loads[0].wait()
     halos = []
     for h in range(SPLIT):
@@ -203,7 +205,7 @@
             copy.start()
 
     signal(met_frm, z_line)
-    signal(met_pix, [z_far, *x_line, partner])
+    signal(met_two, [*z_two, *x_line, partner])
 
     def make_gram(r):
         t_now = t_bf[r]
@@ -255,8 +257,8 @@
         s_bf[0, h] = s_zero_t[h].astype(BF16)
         s_own[h] = s_zero_t[h, rows_of(f), :]
     t_own[...] = temporal_v[rows_of(t_block), :]
-    pl.semaphore_wait(met_pix, 2 + len(x_line))
-    signal(met_core, [partner])
+    pl.semaphore_wait(met_two, len(z_two) + len(x_line) + 1)
+    signal(met_line, [*x_line, partner])
 
     def send_numer(r, h, others):
         for other in others:
@@ -284,6 +286,18 @@
         numer_part[0, h] = dot_nn(t_bf[0], norm_t[h]).astype(BF16)
         send_numer(0, h, [frm_at(dzl, dy) for dzl, dy in FRM_STEPS])
         numer_in[0, h, f] = numer_part[0, h, rows_of(f), :]
+
+    chips, ends = [], []
+    for dx, dzh in CHIP_STEPS:
+        ox, ozh, _ = pix_at(dx, dzh, 0)
+        chips.append((ox, ozh, pix_device(ox, ozh, c)))
+    for dx in (2, 1, 3, 0):
+        for ozh in range(2):
+            ox = lax.rem(x + dx, 4)
+            ends.append((ox, ozh, ((ox * 2 + ozh) * 2 + c, frm_at(2, 0))))
+
+    pl.semaphore_wait(met_line, len(x_line) + 1)
+    signal(met_pix, [partner])
 
     for r in range(ROUNDS):
         last = r == ROUNDS - 1
@@ -307,16 +321,24 @@
             for dzl, dy in FRM_STEPS:
                 remote(mine, mine, at + SHARE + h, (p, frm_at(dzl, dy))).start()
             if last:
-                s_low[h, rows_of(f), :] = low
-
-        numer_t = gram_t = 0.0
+                s_low[y, zl, :, pl.ds(h * PART, PART)] = low
+
+        if last:
+            for target in z_line:
+                remote(s_low.at[y, zl], s_low.at[y, zl], at + LOW, target).start()
+
+        numer_t = second_t = 0.0
         for h in range(SPLIT):
             wait_bytes(s_bf.at[r + 1, h, pl.ds(0, COMP - ROWS)], recv_sem.at[at + SHARE + h])
             s_now = s_bf[r + 1, h]
             numer_t = numer_t + dot_nt(s_now, norm_t[h])
-            gram_t = gram_t + dot_nt(s_now, s_now)
+            if last:
+                second = dot_nn(t_turned[...], s_now).astype(BF16)
+            else:
+                second = s_now
+            second_t = second_t + dot_nt(s_now, second)
         mixed_part[r, :, pl.ds(0, FRM)] = numer_t.astype(BF16)
-        mixed_part[r, :, pl.ds(FRM, COMP)] = gram_t.astype(BF16)
+        mixed_part[r, :, pl.ds(FRM, COMP)] = second_t.astype(BF16)
         remote(
             mixed_part.at[r, rows_of(1 - c, HALF)],
             core_in.at[r],
@@ -327,34 +349,33 @@
         chip_sum = mixed_part[r, rows_of(c, HALF), :].astype(F32) + core_in[r].astype(F32)
         chip_part[r] = chip_sum.astype(BF16)
         if not r:
-            pl.semaphore_wait(met_core, 1)
-        for dx, dzh in CHIP_STEPS:
-            ox, ozh, _ = pix_at(dx, dzh, 0)
+            pl.semaphore_wait(met_pix, 1)
+        for ox, ozh, target in ends if last else chips:
             remote(
                 chip_part.at[r, rows_of(ozh * 4 + ox)],
                 chip_in.at[r, pix_block],
                 at + CHIP,
-                pix_device(ox, ozh, c),
+                target,
             ).start()
-        chip_in[r, pix_block] = chip_part[r, rows_of(pix_block), :]
         if last:
-            for h in range(SPLIT):
-                mine = s_low.at[h, rows_of(f)]
-                for dzl, dy in FRM_STEPS:
-                    remote(mine, mine, at + LOW + h, (p, frm_at(dzl, dy))).start()
-        wait_bytes(chip_in.at[r, pl.ds(0, CHIPS - 1)], recv_sem.at[at + CHIP])
-        total = summed(chip_in.at[r], CHIPS)
-        (denom_t,) = product(
-            total[:, FRM:], [t_bf[r]], t_block, [t_own[...]], [t_bf[r, rows_of(t_block), :]]
-        )
-        t_new = t_own[...] * total[:, :FRM] / (denom_t + epsilon)
-        t_own[...] = t_new
+            wait_bytes(s_low.at[0, pl.ds(0, 3)], recv_sem.at[at + LOW])
+            for target in y_line:
+                remote(s_low.at[y], s_low.at[y], at + LOW + 1, target).start()
         if not last:
+            chip_in[r, pix_block] = chip_part[r, rows_of(pix_block), :]
+            wait_bytes(chip_in.at[r, pl.ds(0, CHIPS - 1)], recv_sem.at[at + CHIP])
+            total = summed(chip_in.at[r], CHIPS)
+            (denom_t,) = product(
+                total[:, FRM:], [t_bf[r]], t_block, [t_own[...]], [t_bf[r, rows_of(t_block), :]]
+            )
+            t_new = t_own[...] * total[:, :FRM] / (denom_t + epsilon)
+            t_own[...] = t_new
             t_bf[r + 1, rows_of(t_block), :] = t_new.astype(BF16)
             mine = t_bf.at[r + 1, rows_of(t_block)]
             for dx, dzh, dc in PIX_STEPS:
                 sem = at + (FAR if dzh else NEAR)
                 remote(mine, mine, sem, pix_device(*pix_at(dx, dzh, dc))).start()
+            remote(t_own, t_across, at + ACROSS, (p, frm_at(2, 0))).start()
             for part, sem, count in ((0, NEAR, CHIPS - 1), (1, FAR, CHIPS)):
                 wait_bytes(t_bf.at[r + 1, pl.ds(0, count * ROWS)], recv_sem.at[at + sem])
                 if part:
@@ -382,18 +403,31 @@
 
             for h in range(SPLIT):
                 numer_in[r + 1, h, f] = numer_part[r + 1, h, rows_of(f), :]
+            t_turned[...] = t_bf[r + 1].T
         else:
-            t_out[rows_of(t_block), :] = t_new
-            mine = t_out.at[rows_of(t_block)]
-            for dx, dzh in CHIP_STEPS:
-                ox, ozh, _ = pix_at(dx, dzh, 0)
-                sem = at + (FAR if dzh else NEAR)
-                remote(mine, mine, sem, pix_device(ox, ozh, c)).start()
+            wait_bytes(t_across, recv_sem.at[at - PHASES + ACROSS])
+            wait_bytes(chip_in.at[r], recv_sem.at[at + CHIP])
+            total = summed(chip_in.at[r], CHIPS)
+            t_across[...] = t_across[...] * total[:, :FRM] / (total[:, FRM:] + epsilon)
+            for _, ozh, target in ends:
+                place = t_out.at[rows_of(t_block)]
+
+                @pl.when(ozh == zh)
+                def _():
+                    remote(t_across, place, at + NEAR, target).start()
+
+                @pl.when(ozh != zh)
+                def _():
+                    remote(t_across, place, at + FAR, target).start()
+
+            wait_bytes(s_low.at[pl.ds(0, 3)], recv_sem.at[at + LOW + 1])
             for h in range(SPLIT):
-                wait_bytes(s_low.at[h, pl.ds(0, COMP - ROWS)], recv_sem.at[at + LOW + h])
-                whole = s_bf[r + 1, h].astype(F32) + s_low[h].astype(F32)
-                s_out[pl.ds(h * PART, PART), :] = whole.T
-            for part, sem, count in ((0, NEAR, 3), (1, FAR, 4)):
+                pixels = pl.ds(h * PART, PART)
+                low = jnp.concatenate(
+                    [s_low[block % 4, block // 4, :, pixels] for block in range(GROUP)], axis=0
+                )
+                s_out[pixels, :] = (s_bf[r + 1, h].astype(F32) + low.astype(F32)).T
+            for part, sem, count in ((0, NEAR, 4), (1, FAR, 4)):
                 wait_bytes(t_out.at[pl.ds(0, count * ROWS)], recv_sem.at[at + sem])
                 group = lax.rem(zh + part, 2)
                 got = t_out.at[pl.ds(pl.multiple_of(c * HALF + group * 64, 64), 64)]
@@ -418,19 +452,20 @@
             (GRAM, gram_in.at[r, pl.ds(0, GROUP - 1)]),
             (CORE_GRAM, gram_own.at[r, :, pl.ds(0, HALF)]),
             (CORE, core_in.at[r]),
-            (CHIP, chip_in.at[r, pl.ds(0, CHIPS - 1)]),
+            (CHIP, chip_in.at[r, pl.ds(0, CHIPS if last else CHIPS - 1)]),
         ]
         for h in range(SPLIT):
             sent.append((NUMER + h, numer_in.at[r, h, pl.ds(0, GROUP - 1)]))
             sent.append((SHARE + h, s_bf.at[r + 1, h, pl.ds(0, COMP - ROWS)]))
         if last:
-            sent += [(LOW + h, s_low.at[h, pl.ds(0, COMP - ROWS)]) for h in range(SPLIT)]
-            sent += [(NEAR, t_out.at[pl.ds(0, 3 * ROWS)]), (FAR, t_out.at[pl.ds(0, 4 * ROWS)])]
+            sent += [(LOW, s_low.at[0, pl.ds(0, 3)]), (LOW + 1, s_low.at[pl.ds(0, 3)])]
+            sent += [(sem, t_out.at[pl.ds(0, 4 * ROWS)]) for sem in (NEAR, FAR)]
             sent += [(RELAY + part, t_out.at[pl.ds(0, 64)]) for part in range(2)]
         else:
             sent += [
                 (NEAR, t_bf.at[r + 1, pl.ds(0, 7 * ROWS)]),
                 (FAR, t_bf.at[r + 1, pl.ds(0, 8 * ROWS)]),
+                (ACROSS, t_across),
             ]
         for sem, ref in sent:
             wait_bytes(ref, send_sem.at[at + sem])
@@ -475,14 +510,16 @@
             pltpu.VMEM((SPLIT, COMP, PART), F32),
             pltpu.VMEM((SPLIT, ROWS, PART), F32),
             pltpu.VMEM((ROWS, FRM), F32),
+            pltpu.VMEM((ROWS, FRM), F32),
             pltpu.VMEM((ROUNDS, COMP, FRM), BF16),
+            pltpu.VMEM((FRM, COMP), BF16),
             pltpu.VMEM((ROUNDS, COMP, HALF), BF16),
             pltpu.VMEM((ROUNDS, GROUP, ROWS, HALF), BF16),
             pltpu.VMEM((ROUNDS, ROWS, COMP), F32),
             pltpu.VMEM((ROUNDS, SPLIT, COMP, PART), BF16),
             pltpu.VMEM((ROUNDS, SPLIT, GROUP, ROWS, PART), BF16),
             pltpu.VMEM((ROUNDS + 1, SPLIT, COMP, PART), BF16),
-            pltpu.VMEM((SPLIT, COMP, PART), BF16),
+            pltpu.VMEM((4, 4, ROWS, PIX), BF16),
             pltpu.VMEM((ROUNDS, COMP, FRM + COMP), BF16),
             pltpu.VMEM((ROUNDS, HALF, FRM + COMP), BF16),
             pltpu.VMEM((ROUNDS, HALF, FRM + COMP), BF16),
@@ -492,7 +529,7 @@
             pltpu.SemaphoreType.DMA((2 * SPLIT,)),
             pltpu.SemaphoreType.DMA((ROUNDS * PHASES,)),
             pltpu.SemaphoreType.DMA((ROUNDS * PHASES,)),
-            pltpu.SemaphoreType.REGULAR((3,)),
+            pltpu.SemaphoreType.REGULAR((4,)),
         ],
         compiler_params=pltpu.CompilerParams(
             collective_id=0, has_side_effects=True, vmem_limit_bytes=40 << 20

time: 78.6 us -> 76.9 us (0.978)
  Pallas kernels: 77.9 us -> 76.2 us
    pallas_call x1, Pallas kernels: 77 us -> 75.3 us  [on_device(): pl.pallas_call(kernel, out_shape=shapes, in_specs=[hbm] * 6, out_specs=(v...]
where the time goes in v5:
time: 76.9 us; the launch traced here: 76.8 us
  Pallas kernels  76.2 us (99%)
    pallas_call x1, Pallas kernels, on_device(): pl.pallas_call(kernel, out_shape=shapes, in_specs=[hbm] * 6, out_specs=(v...  75.3 us

profile of v5, /device:TPU:1, one launch (start us, length us, event | category | flops | bytes accessed | tf_op | source)
XLA Modules:
  0.0 76.8 jit_solution(11265228328807161588)
XLA Ops:
  0.6 75.3 %shard_map.77 = (f32[512,256]{1,0:T(8,128)S(1)}, f32[256,256]{1,0:T(8,128)S(1)}) custom-call(bf16[512,256]{1,0:T(8,128)(2,1)} %movie_hbm.1, f32[257]{0:T(512)} %taps_hbm.1, f32[512]{0:T(512)} %scale_hbm.1, f32[512]{0:T(512)} %base_hbm.1, f32[512,256]{1,0:T(8,128)} %spatial_hbm.1, f32[256,256]{1,0:T(8,128)} %temporal_hbm.1), custom_call_target="tpu_custom_call" | custom-call | tf_op jit(solution)/shard_map/pallas_call | solution.py:496
  75.9 0.9 %shard_map.78 = (f32[512,256]{1,0:T(8,128)}, f32[256,256]{1,0:T(8,128)}) custom-call(f32[512,256]{1,0:T(8,128)S(1)} %get-tuple-element.4.s_v, f32[256,256]{1,0:T(8,128)S(1)} %get-tuple-element.5.t_v), custom_call_target="tpu_custom_call" | custom-call | tf_op jit(solution)/shard_map/pallas_call | solution.py:538

commit v6 on v5

--- a/solution.py
+++ b/solution.py
@@ -20,7 +20,7 @@
 COMP = 256
 ROWS = COMP // GROUP
 HALO = 128
-SPLIT = 2
+SPLIT = 1
 PART = PIX // SPLIT
 HALF = COMP // 2
 TAPS = 257
@@ -298,6 +298,31 @@
 
     pl.semaphore_wait(met_line, len(x_line) + 1)
     signal(met_pix, [partner])
+
+    def left(r, *names):
+        last = r == ROUNDS - 1
+        temporal_rows = t_out if last else t_bf.at[ROUNDS - 1]
+        refs = {
+            GRAM: gram_in.at[r, pl.ds(0, GROUP - 1)],
+            CORE_GRAM: gram_own.at[r, :, pl.ds(0, HALF)],
+            CORE: core_in.at[r],
+            CHIP: chip_in.at[r, pl.ds(0, CHIPS if last else CHIPS - 1)],
+            NEAR: temporal_rows.at[pl.ds(0, (4 if last else 7) * ROWS)],
+            FAR: temporal_rows.at[pl.ds(0, (4 if last else 8) * ROWS)],
+            LOW: s_low.at[0, pl.ds(0, 3)],
+            LOW + 1: s_low.at[pl.ds(0, 3)],
+            ACROSS: t_across,
+            RELAY: t_out.at[pl.ds(0, 64)],
+            RELAY + 1: t_out.at[pl.ds(0, 64)],
+        }
+        for h in range(SPLIT):
+            refs[NUMER + h] = numer_in.at[r, h, pl.ds(0, GROUP - 1)]
+            refs[SHARE + h] = s_bf.at[r + 1, h, pl.ds(0, COMP - ROWS)]
+        for name in names:
+            wait_bytes(refs[name], send_sem.at[r * PHASES + name])
+
+    spatial_phases = [GRAM, CORE_GRAM, *(NUMER + h for h in range(SPLIT))]
+    spatial_phases += [SHARE + h for h in range(SPLIT)]
 
     for r in range(ROUNDS):
         last = r == ROUNDS - 1
@@ -361,6 +386,19 @@
             wait_bytes(s_low.at[0, pl.ds(0, 3)], recv_sem.at[at + LOW])
             for target in y_line:
                 remote(s_low.at[y], s_low.at[y], at + LOW + 1, target).start()
+        if not r:
+
+            @pl.when(has_right)
+            def _():
+                for copy in halos[0::2]:
+                    copy.wait_send()
+
+            @pl.when(has_left)
+            def _():
+                for copy in halos[1::2]:
+                    copy.wait_send()
+
+        left(r, *spatial_phases, CORE)
         if not last:
             chip_in[r, pix_block] = chip_part[r, rows_of(pix_block), :]
             wait_bytes(chip_in.at[r, pl.ds(0, CHIPS - 1)], recv_sem.at[at + CHIP])
@@ -420,6 +458,8 @@
                 def _():
                     remote(t_across, place, at + FAR, target).start()
 
+            left(r - 1, CHIP, NEAR, FAR, ACROSS)
+            left(r, CHIP, LOW, LOW + 1)
             wait_bytes(s_low.at[pl.ds(0, 3)], recv_sem.at[at + LOW + 1])
             for h in range(SPLIT):
                 pixels = pl.ds(h * PART, PART)
@@ -434,41 +474,7 @@
                 remote(got, got, at + RELAY + part, pix_device(x, zh, 1 - c)).start()
             for part in range(2):
                 wait_bytes(t_out.at[pl.ds(0, 64)], recv_sem.at[at + RELAY + part])
-
-    @pl.when(has_right)
-    def _():
-        for copy in halos[0::2]:
-            copy.wait_send()
-
-    @pl.when(has_left)
-    def _():
-        for copy in halos[1::2]:
-            copy.wait_send()
-
-    for r in range(ROUNDS):
-        last = r == ROUNDS - 1
-        at = r * PHASES
-        sent = [
-            (GRAM, gram_in.at[r, pl.ds(0, GROUP - 1)]),
-            (CORE_GRAM, gram_own.at[r, :, pl.ds(0, HALF)]),
-            (CORE, core_in.at[r]),
-            (CHIP, chip_in.at[r, pl.ds(0, CHIPS if last else CHIPS - 1)]),
-        ]
-        for h in range(SPLIT):
-            sent.append((NUMER + h, numer_in.at[r, h, pl.ds(0, GROUP - 1)]))
-            sent.append((SHARE + h, s_bf.at[r + 1, h, pl.ds(0, COMP - ROWS)]))
-        if last:
-            sent += [(LOW, s_low.at[0, pl.ds(0, 3)]), (LOW + 1, s_low.at[pl.ds(0, 3)])]
-            sent += [(sem, t_out.at[pl.ds(0, 4 * ROWS)]) for sem in (NEAR, FAR)]
-            sent += [(RELAY + part, t_out.at[pl.ds(0, 64)]) for part in range(2)]
-        else:
-            sent += [
-                (NEAR, t_bf.at[r + 1, pl.ds(0, 7 * ROWS)]),
-                (FAR, t_bf.at[r + 1, pl.ds(0, 8 * ROWS)]),
-                (ACROSS, t_across),
-            ]
-        for sem, ref in sent:
-            wait_bytes(ref, send_sem.at[at + sem])
+            left(r, NEAR, FAR, RELAY, RELAY + 1)
 
 
 def hand_on(s_v, t_v, s_out, t_out, sem):

time: 76.9 us -> 76 us (0.988)
  Pallas kernels: 76.2 us -> 75.3 us
    pallas_call x1, Pallas kernels: 75.3 us -> 74.4 us  [on_device(): pl.pallas_call(kernel, out_shape=shapes, in_specs=[hbm] * 6, out_specs=(v...]
where the time goes in v6:
time: 76 us; the launch traced here: 75.9 us
  Pallas kernels  75.3 us (99%)
    pallas_call x1, Pallas kernels, on_device(): pl.pallas_call(kernel, out_shape=shapes, in_specs=[hbm] * 6, out_specs=(v...  74.4 us

profile of v6, /device:TPU:1, one launch (start us, length us, event | category | flops | bytes accessed | tf_op | source)
XLA Modules:
  0.0 75.9 jit_solution(5189157813687877792)
XLA Ops:
  0.6 74.4 %shard_map.77 = (f32[512,256]{1,0:T(8,128)S(1)}, f32[256,256]{1,0:T(8,128)S(1)}) custom-call(bf16[512,256]{1,0:T(8,128)(2,1)} %movie_hbm.1, f32[257]{0:T(512)} %taps_hbm.1, f32[512]{0:T(512)} %scale_hbm.1, f32[512]{0:T(512)} %base_hbm.1, f32[512,256]{1,0:T(8,128)} %spatial_hbm.1, f32[256,256]{1,0:T(8,128)} %temporal_hbm.1), custom_call_target="tpu_custom_call" | custom-call | tf_op jit(solution)/shard_map/pallas_call | solution.py:502
  75.0 0.9 %shard_map.78 = (f32[512,256]{1,0:T(8,128)}, f32[256,256]{1,0:T(8,128)}) custom-call(f32[512,256]{1,0:T(8,128)S(1)} %get-tuple-element.4.s_v, f32[256,256]{1,0:T(8,128)S(1)} %get-tuple-element.5.t_v), custom_call_target="tpu_custom_call" | custom-call | tf_op jit(solution)/shard_map/pallas_call | solution.py:544

commit v7 on v6

--- a/solution.py
+++ b/solution.py
@@ -30,10 +30,7 @@
     return sorted(steps, key=lambda step: -hops(*step))
 
 
-FRM_STEPS = far_first(
-    [(dzl, dy) for dzl in range(4) for dy in range(4) if dzl or dy],
-    lambda dzl, dy: dzl + min(dy, 4 - dy),
-)
+Y_STEPS = (2, 1, 3, 0)
 CHIP_STEPS = far_first(
     [(dx, dzh) for dx in range(4) for dzh in range(2) if dx or dzh],
     lambda dx, dzh: min(dx, 4 - dx) + 4 * dzh,
@@ -114,11 +111,21 @@
     def frm_at(dzl, dy):
         return lax.rem(zl + dzl, 4) * 4 + lax.rem(y + dy, 4)
 
+    mirrored, across, beside = 3 - zl, lax.rem(zl + 2, 4), zl + 1 - 2 * lax.rem(zl, 2)
+
+    def in_plane(plane, steps=Y_STEPS):
+        return [plane * 4 + lax.rem(y + dy, 4) for dy in steps]
+
+    planes = (mirrored, across, beside, zl)
+    frm_others = [
+        plane * 4 + lax.rem(y + dy, 4) for dy in Y_STEPS for plane in (planes if dy else planes[:3])
+    ]
+
     barrier = pltpu.get_barrier_semaphore()
     x_line = [pix_device(*pix_at(dx, 0, 0)) for dx in (2, 1, 3)]
     partner = pix_device(x, zh, 1 - c)
     z_two = [(pix_device(x, 1 - zh, c)[0], frm_at(2, 0)), (p, frm_at(2, 0))]
-    z_line = [(p, frm_at(dzl, 0)) for dzl in (3, 2, 1)]
+    z_line = [(p, plane * 4 + y) for plane in (mirrored, across, beside)]
     y_line = [(p, frm_at(0, dy)) for dy in (2, 1, 3)]
 
     def signal(sem, targets):
@@ -213,8 +220,7 @@
         gram_part[r] = dot_nt(t_now, t_half).astype(BF16)
 
     def send_gram(r):
-        for dzl, dy in FRM_STEPS:
-            other = frm_at(dzl, dy)
+        for other in frm_others:
             remote(
                 gram_part.at[r, rows_of(other)], gram_in.at[r, f], r * PHASES + GRAM, (p, other)
             ).start()
@@ -284,7 +290,7 @@
         scaled = scale_v[pixels][None] * mixed + base_v[pixels][None]
         norm_t[h] = jnp.maximum(scaled, 0.0).astype(BF16)
         numer_part[0, h] = dot_nn(t_bf[0], norm_t[h]).astype(BF16)
-        send_numer(0, h, [frm_at(dzl, dy) for dzl, dy in FRM_STEPS])
+        send_numer(0, h, frm_others)
         numer_in[0, h, f] = numer_part[0, h, rows_of(f), :]
 
     chips, ends = [], []
@@ -343,8 +349,8 @@
             high, low = split(s_new)
             s_bf[r + 1, h, rows_of(f), :] = high
             mine = s_bf.at[r + 1, h, rows_of(f)]
-            for dzl, dy in FRM_STEPS:
-                remote(mine, mine, at + SHARE + h, (p, frm_at(dzl, dy))).start()
+            for other in frm_others:
+                remote(mine, mine, at + SHARE + h, (p, other)).start()
             if last:
                 s_low[y, zl, :, pl.ds(h * PART, PART)] = low
 
@@ -422,22 +428,19 @@
                 group = lax.rem(zh + part, 2)
                 spans = [pl.ds(pl.multiple_of(b * HALF + group * 64, 64), 64) for b in range(2)]
                 t_rows = jnp.concatenate([t_bf[r + 1, span, :] for span in spans], axis=0)
-                first = lax.rem(zl + group, 2)
+                odd = lax.rem(zl + group, 2)
+                far_plane = across + odd * (mirrored - across)
+                near_plane = zl + odd * (beside - zl)
                 for h in range(SPLIT):
                     rows = dot_nn(t_rows, norm_t[h]).astype(BF16)
                     for b, span in enumerate(spans):
                         numer_part[r + 1, h, span, :] = rows[b * 64 : (b + 1) * 64]
                 for h in range(SPLIT):
-                    for i in (2, 0):
-                        for dy in (2, 1, 3, 0):
-                            other = frm_at(first + i, dy)
-                            if i or dy:
-                                send_numer(r + 1, h, [other])
-                            else:
-
-                                @pl.when(first > 0)
-                                def _():
-                                    send_numer(r + 1, h, [other])
+                    send_numer(r + 1, h, in_plane(far_plane) + in_plane(near_plane, Y_STEPS[:3]))
+
+                    @pl.when(odd > 0)
+                    def _():
+                        send_numer(r + 1, h, in_plane(near_plane, Y_STEPS[3:]))
 
             for h in range(SPLIT):
                 numer_in[r + 1, h, f] = numer_part[r + 1, h, rows_of(f), :]

time: 76 us -> 74.9 us (0.986)
  Pallas kernels: 75.3 us -> 74.2 us
    pallas_call x1, Pallas kernels: 74.4 us -> 73.3 us  [on_device(): pl.pallas_call(kernel, out_shape=shapes, in_specs=[hbm] * 6, out_specs=(v...]
where the time goes in v7:
time: 74.9 us; the launch traced here: 74.8 us
  Pallas kernels  74.2 us (99%)
    pallas_call x1, Pallas kernels, on_device(): pl.pallas_call(kernel, out_shape=shapes, in_specs=[hbm] * 6, out_specs=(v...  73.3 us

profile of v7, /device:TPU:1, one launch (start us, length us, event | category | flops | bytes accessed | tf_op | source)
XLA Modules:
  0.0 74.8 jit_solution(17394453189717422814)
XLA Ops:
  0.6 73.3 %shard_map.77 = (f32[512,256]{1,0:T(8,128)S(1)}, f32[256,256]{1,0:T(8,128)S(1)}) custom-call(bf16[512,256]{1,0:T(8,128)(2,1)} %movie_hbm.1, f32[257]{0:T(512)} %taps_hbm.1, f32[512]{0:T(512)} %scale_hbm.1, f32[512]{0:T(512)} %base_hbm.1, f32[512,256]{1,0:T(8,128)} %spatial_hbm.1, f32[256,256]{1,0:T(8,128)} %temporal_hbm.1), custom_call_target="tpu_custom_call" | custom-call | tf_op jit(solution)/shard_map/pallas_call | solution.py:505
  73.9 0.9 %shard_map.78 = (f32[512,256]{1,0:T(8,128)}, f32[256,256]{1,0:T(8,128)}) custom-call(f32[512,256]{1,0:T(8,128)S(1)} %get-tuple-element.4.s_v, f32[256,256]{1,0:T(8,128)S(1)} %get-tuple-element.5.t_v), custom_call_target="tpu_custom_call" | custom-call | tf_op jit(solution)/shard_map/pallas_call | solution.py:547

commit v8 on v7

--- a/solution.py
+++ b/solution.py
@@ -354,10 +354,6 @@
             if last:
                 s_low[y, zl, :, pl.ds(h * PART, PART)] = low
 
-        if last:
-            for target in z_line:
-                remote(s_low.at[y, zl], s_low.at[y, zl], at + LOW, target).start()
-
         numer_t = second_t = 0.0
         for h in range(SPLIT):
             wait_bytes(s_bf.at[r + 1, h, pl.ds(0, COMP - ROWS)], recv_sem.at[at + SHARE + h])
@@ -376,6 +372,9 @@
             at + CORE,
             pix_device(x, zh, 1 - c),
         ).start()
+        if last:
+            for target in z_line:
+                remote(s_low.at[y, zl], s_low.at[y, zl], at + LOW, target).start()
         wait_bytes(core_in.at[r], recv_sem.at[at + CORE])
         chip_sum = mixed_part[r, rows_of(c, HALF), :].astype(F32) + core_in[r].astype(F32)
         chip_part[r] = chip_sum.astype(BF16)
@@ -461,6 +460,11 @@
                 def _():
                     remote(t_across, place, at + FAR, target).start()
 
+            for part, sem, count in ((0, NEAR, 4), (1, FAR, 4)):
+                wait_bytes(t_out.at[pl.ds(0, count * ROWS)], recv_sem.at[at + sem])
+                group = lax.rem(zh + part, 2)
+                got = t_out.at[pl.ds(pl.multiple_of(c * HALF + group * 64, 64), 64)]
+                remote(got, got, at + RELAY + part, pix_device(x, zh, 1 - c)).start()
             left(r - 1, CHIP, NEAR, FAR, ACROSS)
             left(r, CHIP, LOW, LOW + 1)
             wait_bytes(s_low.at[pl.ds(0, 3)], recv_sem.at[at + LOW + 1])
@@ -470,11 +474,6 @@
                     [s_low[block % 4, block // 4, :, pixels] for block in range(GROUP)], axis=0
                 )
                 s_out[pixels, :] = (s_bf[r + 1, h].astype(F32) + low.astype(F32)).T
-            for part, sem, count in ((0, NEAR, 4), (1, FAR, 4)):
-                wait_bytes(t_out.at[pl.ds(0, count * ROWS)], recv_sem.at[at + sem])
-                group = lax.rem(zh + part, 2)
-                got = t_out.at[pl.ds(pl.multiple_of(c * HALF + group * 64, 64), 64)]
-                remote(got, got, at + RELAY + part, pix_device(x, zh, 1 - c)).start()
             for part in range(2):
                 wait_bytes(t_out.at[pl.ds(0, 64)], recv_sem.at[at + RELAY + part])
             left(r, NEAR, FAR, RELAY, RELAY + 1)

time: 74.9 us -> 74.4 us (level)
  no operation moved by 1% of the time
where the time goes in v8:
time: 74.4 us; the launch traced here: 74.3 us
  Pallas kernels  73.7 us (99%)
    pallas_call x1, Pallas kernels, on_device(): pl.pallas_call(kernel, out_shape=shapes, in_specs=[hbm] * 6, out_specs=(v...  72.8 us

profile of v8, /device:TPU:1, one launch (start us, length us, event | category | flops | bytes accessed | tf_op | source)
XLA Modules:
  0.0 74.3 jit_solution(9492809195788522600)
XLA Ops:
  0.6 72.8 %shard_map.77 = (f32[512,256]{1,0:T(8,128)S(1)}, f32[256,256]{1,0:T(8,128)S(1)}) custom-call(bf16[512,256]{1,0:T(8,128)(2,1)} %movie_hbm.1, f32[257]{0:T(512)} %taps_hbm.1, f32[512]{0:T(512)} %scale_hbm.1, f32[512]{0:T(512)} %base_hbm.1, f32[512,256]{1,0:T(8,128)} %spatial_hbm.1, f32[256,256]{1,0:T(8,128)} %temporal_hbm.1), custom_call_target="tpu_custom_call" | custom-call | tf_op jit(solution)/shard_map/pallas_call | solution.py:504
  73.4 0.9 %shard_map.78 = (f32[512,256]{1,0:T(8,128)}, f32[256,256]{1,0:T(8,128)}) custom-call(f32[512,256]{1,0:T(8,128)S(1)} %get-tuple-element.4.s_v, f32[256,256]{1,0:T(8,128)S(1)} %get-tuple-element.5.t_v), custom_call_target="tpu_custom_call" | custom-call | tf_op jit(solution)/shard_map/pallas_call | solution.py:546

commit v9 on v8

--- a/solution.py
+++ b/solution.py
@@ -54,16 +54,15 @@
     return high, (value - high.astype(F32)).astype(BF16)
 
 
-def product(gram, wholes, block, owns, own_copies):
-    terms = jnp.concatenate(split(gram), axis=0)
+def product(gram, whole):
+    both = dot_nn(jnp.concatenate(split(gram), axis=0), whole)
+    return both[:ROWS] + both[ROWS:]
+
+
+def diagonal_of(gram, block):
     row = lax.broadcasted_iota(jnp.int32, gram.shape, 0)
     column = lax.broadcasted_iota(jnp.int32, gram.shape, 1)
-    diagonal = jnp.sum(jnp.where(column == row + block * ROWS, gram, 0.0), axis=1, keepdims=True)
-    results = []
-    for whole, own, copy in zip(wholes, owns, own_copies):
-        both = dot_nn(terms, whole)
-        results.append(both[:ROWS] + both[ROWS:] + diagonal * (own - copy.astype(F32)))
-    return results
+    return jnp.sum(jnp.where(column == row + block * ROWS, gram, 0.0), axis=1, keepdims=True)
 
 
 def rows_of(index, count=ROWS):
@@ -233,7 +232,16 @@
         mine = gram_own.at[r, :, half]
         copy = remote(mine, mine, r * PHASES + CORE_GRAM, pix_device(x, zh, 1 - c))
         copy.start()
+        parts = [product(gram_own[r, :, half], s_bf[r, h, rows_of(c, HALF), :]) for h in range(SPLIT)]
         copy.wait_recv()
+        rest = pl.ds(pl.multiple_of((1 - c) * HALF, HALF), HALF)
+        diagonal = diagonal_of(gram_own[r], f)
+        denoms = []
+        for h in range(SPLIT):
+            denom = parts[h] + product(gram_own[r, :, rest], s_bf[r, h, rows_of(1 - c, HALF), :])
+            error = s_own[h] - s_bf[r, h, rows_of(f), :].astype(F32)
+            denoms.append(denom + diagonal * error)
+        return denoms
 
     loads[1].wait()
     t_bf[0] = temporal_v[...].astype(BF16)
@@ -333,14 +341,7 @@
     for r in range(ROUNDS):
         last = r == ROUNDS - 1
         at = r * PHASES
-        finish_gram(r)
-        denoms = product(
-            gram_own[r],
-            [s_bf[r, h] for h in range(SPLIT)],
-            f,
-            [s_own[h] for h in range(SPLIT)],
-            [s_bf[r, h, rows_of(f), :] for h in range(SPLIT)],
-        )
+        denoms = finish_gram(r)
         for h in range(SPLIT):
             wait_bytes(numer_in.at[r, h, pl.ds(0, GROUP - 1)], recv_sem.at[at + NUMER + h])
             numer = summed(numer_in.at[r, h], GROUP)
@@ -408,9 +409,9 @@
             chip_in[r, pix_block] = chip_part[r, rows_of(pix_block), :]
             wait_bytes(chip_in.at[r, pl.ds(0, CHIPS - 1)], recv_sem.at[at + CHIP])
             total = summed(chip_in.at[r], CHIPS)
-            (denom_t,) = product(
-                total[:, FRM:], [t_bf[r]], t_block, [t_own[...]], [t_bf[r, rows_of(t_block), :]]
-            )
+            gram_t = total[:, FRM:]
+            error = t_own[...] - t_bf[r, rows_of(t_block), :].astype(F32)
+            denom_t = product(gram_t, t_bf[r]) + diagonal_of(gram_t, t_block) * error
             t_new = t_own[...] * total[:, :FRM] / (denom_t + epsilon)
             t_own[...] = t_new
             t_bf[r + 1, rows_of(t_block), :] = t_new.astype(BF16)

time: 74.4 us -> 74.5 us (level)
  no operation moved by 1% of the time
where the time goes in v9:
time: 74.5 us; the launch traced here: 74.4 us
  Pallas kernels  73.7 us (99%)
    pallas_call x1, Pallas kernels, on_device(): pl.pallas_call(kernel, out_shape=shapes, in_specs=[hbm] * 6, out_specs=(v...  72.8 us

profile of v9, /device:TPU:1, one launch (start us, length us, event | category | flops | bytes accessed | tf_op | source)
XLA Modules:
  0.0 74.4 jit_solution(17762610639396647197)
XLA Ops:
  0.6 72.8 %shard_map.77 = (f32[512,256]{1,0:T(8,128)S(1)}, f32[256,256]{1,0:T(8,128)S(1)}) custom-call(bf16[512,256]{1,0:T(8,128)(2,1)} %movie_hbm.1, f32[257]{0:T(512)} %taps_hbm.1, f32[512]{0:T(512)} %scale_hbm.1, f32[512]{0:T(512)} %base_hbm.1, f32[512,256]{1,0:T(8,128)} %spatial_hbm.1, f32[256,256]{1,0:T(8,128)} %temporal_hbm.1), custom_call_target="tpu_custom_call" | custom-call | tf_op jit(solution)/shard_map/pallas_call | solution.py:505
  73.5 0.9 %shard_map.78 = (f32[512,256]{1,0:T(8,128)}, f32[256,256]{1,0:T(8,128)}) custom-call(f32[512,256]{1,0:T(8,128)S(1)} %get-tuple-element.4.s_v, f32[256,256]{1,0:T(8,128)S(1)} %get-tuple-element.5.t_v), custom_call_target="tpu_custom_call" | custom-call | tf_op jit(solution)/shard_map/pallas_call | solution.py:547
